TPU v7x, 32 devices: a whole 2x2x4 slice. The times are simulated.
32 devices in a mesh: grp: 8 (over z, x), dev: 4 (over y, core).
Axes of the slice: x: 2, y: 2, z: 4, core: 2. Of those that a mesh axis runs over, the one named last changes fastest.
Arguments:
- node_src: bfloat16 [4096, 1024], P(('grp', 'dev'))
- hub_feat: bfloat16 [4096, 1024], P(('grp', 'dev'))
- w_query: bfloat16 [1024, 1024], replicated, may hold values from -0.1875 to 0.1875
- w_key: bfloat16 [1024, 1024], replicated, may hold values from -0.1875 to 0.1875
- w_value: bfloat16 [1024, 1024], replicated, may hold values from -0.1875 to 0.1875
- w_out: bfloat16 [1024, 1024], replicated, may hold values from -0.75 to 0.75
- w_att: bfloat16 [16, 16, 64, 64], replicated, may hold values from -0.75 to 0.75
- w_msg: bfloat16 [16, 16, 64, 64], replicated, may hold values from -0.75 to 0.75
- relation_prior: float32 [16, 16], replicated, may hold values from 0.5 to 2
- block_src: int32 [32, 40], P(('grp', 'dev')), may hold values from 0 to 7
- block_dst: int32 [32, 40], P(('grp', 'dev')), may hold values from 0 to 3
- block_type: int32 [32, 40], P(('grp', 'dev')), may hold values from 0 to 15
- block_count: int32 [32], P(('grp', 'dev')), may hold values from 20 to 40, as said below
Outputs:
- hub_out: bfloat16 [4096, 1024], P(('grp', 'dev'))
Inputs may be any that keep to these rules, and one draw needn't show every extreme that they name: `block_count`: some device uses all 40 slots; every hub tile of a group is the target of some used block of that group.
All inputs are finite; a program needn't handle non-finite values.
Results may differ from a plain program's by a relative error of at most 0.018.
The roundings to bfloat16 on the way count: a program that leaves them out, or rounds other values in their place, can miss the bound.
Values may be sent and summed in bfloat16 or wider, within the bound.
No kernel may reach another device: no remote copies, remote signals or barrier semaphores. Data moves between devices by JAX's collectives and lax.ppermute only.
A program may use at most 128 MiB of HBM per device.

v0:
```python
import jax
import jax.numpy as jnp
from jax import lax
from jax.sharding import PartitionSpec as P


def body(
    node_src,
    hub_feat,
    w_query,
    w_key,
    w_value,
    w_out,
    w_att,
    w_msg,
    relation_prior,
    block_src,
    block_dst,
    block_type,
    block_count,
):
    owners = lax.axis_size("dev")
    tile_rows = hub_feat.shape[0]
    width = hub_feat.shape[1]
    heads = relation_prior.shape[1]
    head_dim = width // heads
    group_hubs = owners * tile_rows
    queries = jnp.dot(hub_feat, w_query, preferred_element_type=jnp.float32).astype(jnp.bfloat16)
    all_queries = lax.all_gather(queries, "dev", axis=0, tiled=True)
    w_both = jnp.concatenate([w_key, w_value], axis=1)
    own_kv = jnp.dot(node_src, w_both, preferred_element_type=jnp.float32).astype(jnp.bfloat16)
    keyval = lax.all_gather(own_kv, "grp", axis=0, tiled=True)
    scale_root = jnp.sqrt(jnp.float32(head_dim))

    def one_block(slot, carry):
        highest, denom, total = carry
        src_tile = block_src[0, slot]
        dst_tile = block_dst[0, slot]
        rtype = block_type[0, slot]
        src_rows = lax.dynamic_slice_in_dim(keyval, src_tile * tile_rows, tile_rows, 0)
        keys = src_rows[:, :width].reshape(tile_rows, heads, head_dim)
        values = src_rows[:, width:].reshape(tile_rows, heads, head_dim)
        key_rel = jnp.einsum(
            "shd,hde->she", keys, w_att[rtype], preferred_element_type=jnp.float32
        ).astype(jnp.bfloat16)
        message = jnp.einsum(
            "shd,hde->she", values, w_msg[rtype], preferred_element_type=jnp.float32
        ).astype(jnp.bfloat16)
        start = dst_tile * tile_rows
        tile_q = lax.dynamic_slice_in_dim(all_queries, start, tile_rows, 0).reshape(
            tile_rows, heads, head_dim
        )
        scores = jnp.einsum("thd,shd->hts", tile_q, key_rel, preferred_element_type=jnp.float32)
        scores = scores * (relation_prior[rtype] / scale_root)[:, None, None]
        old_top = lax.dynamic_slice_in_dim(highest, start, tile_rows, 0)
        new_top = jnp.maximum(old_top, scores.max(axis=2).T)
        factor = jnp.exp(old_top - new_top)
        weight = jnp.exp(scores - new_top.T[:, :, None])
        summed = jnp.einsum(
            "hts,she->the", weight.astype(jnp.bfloat16), message, preferred_element_type=jnp.float32
        ).reshape(tile_rows, width)
        old_d = lax.dynamic_slice_in_dim(denom, start, tile_rows, 0)
        old_t = lax.dynamic_slice_in_dim(total, start, tile_rows, 0)
        highest = lax.dynamic_update_slice_in_dim(highest, new_top, start, 0)
        denom = lax.dynamic_update_slice_in_dim(
            denom, old_d * factor + weight.sum(axis=2).T, start, 0
        )
        total = lax.dynamic_update_slice_in_dim(
            total, old_t * jnp.repeat(factor, head_dim, axis=1) + summed, start, 0
        )
        return (highest, denom, total)

    init = (
        jnp.full((group_hubs, heads), -1e30, jnp.float32),
        jnp.zeros((group_hubs, heads), jnp.float32),
        jnp.zeros((group_hubs, width), jnp.float32),
    )
    highest, denom, total = lax.fori_loop(0, block_count[0], one_block, init)
    overall = lax.pmax(highest.astype(jnp.bfloat16), "dev").astype(highest.dtype)
    factor = jnp.exp(highest - overall)
    own_total, own_denom = (
        lax.psum_scatter(
            (total * jnp.repeat(factor, head_dim, axis=1)).astype(jnp.bfloat16),
            "dev",
            scatter_dimension=0,
            tiled=True,
        ).astype(jnp.float32),
        lax.psum_scatter(
            (denom * factor).astype(jnp.bfloat16), "dev", scatter_dimension=0, tiled=True
        ).astype(jnp.float32),
    )
    aggregate = (own_total / jnp.repeat(own_denom, head_dim, axis=1)).astype(jnp.bfloat16)
    return jnp.dot(aggregate, w_out, preferred_element_type=jnp.float32).astype(jnp.bfloat16)


def solution(mesh):
    placed = (
        P(("grp", "dev"), None),
        P(("grp", "dev"), None),
        P(),
        P(),
        P(),
        P(),
        P(),
        P(),
        P(),
        P(("grp", "dev"), None),
        P(("grp", "dev"), None),
        P(("grp", "dev"), None),
        P(("grp", "dev")),
    )
    return jax.shard_map(
        body, mesh=mesh, in_specs=placed, out_specs=P(("grp", "dev"), None), check_vma=False
    )
```

profile of v0, /device:TPU:0, one launch (start us, length us, event | category | flops | bytes accessed | tf_op | source)
XLA Modules:
  0.0 891.3 jit_solution(7226197442229210296)
XLA Ops:
  10.3 4.4 fusion.30
  14.7 15.1 %all-gather.3.cloned.1.call-done = bf16[512,1024]{1,0:T(8,128)(2,1)} async-done(((bf16[128,1024]{1,0:T(8,128)(2,1)}), bf16[512,1024]{1,0:T(8,128)(2,1)}) %all-gather.3.cloned.1.call-update) | async-done | bytes 1048592 | tf_op jit(solution)/shard_map/all_gather | solution.py:29
  29.8 77.1 %all-gather.5.cloned.1.call-done = bf16[1024,2048]{0,1:T(8,128)(2,1)} async-done(((bf16[128,2048]{0,1:T(8,128)(2,1)}), bf16[1024,2048]{0,1:T(8,128)(2,1)}) %all-gather.5.cloned.1.call-update) | async-done | bytes 4194320 | tf_op jit(solution)/shard_map/all_gather | solution.py:32
  108.5 411.9 %while.14 = (s32[]{:T(128)}, f32[512,16]{0,1:T(8,128)S(1)}, f32[512,16]{0,1:T(8,128)S(1)}, f32[512,1024]{0,1:T(8,128)}, s32[]{:T(128)}, /*index=5*/s32[1,40]{1,0...) while((s32[]{:T(128)}, f32[512,16]{0,1:T(8,128)S(1)}, ...), condition=%wide.region_3.0_spmd, body=%wide.region_0.0_spmd.sunk | while | flops 102766624 | bytes 8774229 | solution.py:78
  122.1 2.2 fusion.77
  124.3 2.1 constant_dynamic-update-slice_fusion.3
  140.0 2.2 fusion.77
  142.2 2.1 constant_dynamic-update-slice_fusion.3
  157.8 2.2 fusion.77
  160.0 2.1 constant_dynamic-update-slice_fusion.3
  175.7 2.2 fusion.77
  177.9 2.1 constant_dynamic-update-slice_fusion.3
  193.6 2.2 fusion.77
  195.8 2.1 constant_dynamic-update-slice_fusion.3
  211.5 2.2 fusion.77
  213.7 2.1 constant_dynamic-update-slice_fusion.3
  229.4 2.2 fusion.77
  231.6 2.1 constant_dynamic-update-slice_fusion.3
  247.3 2.2 fusion.77
  249.5 2.1 constant_dynamic-update-slice_fusion.3
  265.2 2.2 fusion.77
  267.4 2.1 constant_dynamic-update-slice_fusion.3
  283.0 2.2 fusion.77
  285.2 2.1 constant_dynamic-update-slice_fusion.3
  300.9 2.2 fusion.77
  303.1 2.1 constant_dynamic-update-slice_fusion.3
  318.8 2.2 fusion.77
  336.7 2.2 fusion.77
  354.6 2.2 fusion.77
  356.8 2.1 constant_dynamic-update-slice_fusion.3
  372.4 2.2 fusion.77
  374.6 2.1 constant_dynamic-update-slice_fusion.3
  390.3 2.2 fusion.77
  408.2 2.2 fusion.77
  410.4 2.1 constant_dynamic-update-slice_fusion.3
  426.1 2.2 fusion.77
  428.3 2.1 constant_dynamic-update-slice_fusion.3
  444.0 2.2 fusion.77
  446.2 2.1 constant_dynamic-update-slice_fusion.3
  461.9 2.2 fusion.77
  464.0 2.1 constant_dynamic-update-slice_fusion.3
  479.7 2.2 fusion.77
  497.6 2.2 fusion.77
  515.5 2.2 fusion.77
  520.5 81.0 %pmax.7 = bf16[512,16]{0,1:T(8,128)(2,1)S(1)} all-reduce(bf16[512,16]{0,1:T(8,128)(2,1)S(1)} %convert_element_type.51), channel_id=1, replica_groups=mesh['grp'=8,'dev'=4] {'dev'}, use_global_device_ids=true, to_apply=%region_4.0 | all-reduce | flops 8192 | bytes 32768 | tf_op jit(solution)/shard_map/pmax | solution.py:79
  605.5 247.8 %reduce-scatter.9.cloned.1.call-done = bf16[128,16]{1,0:T(8,128)(2,1)} async-done(((bf16[512,16]{1,0:T(8,128)(2,1)}), bf16[128,16]{1,0:T(8,128)(2,1)}) %reduce-scatter.9.cloned.1.call-update) | async-done | bytes 4112
  854.1 26.7 %reduce-scatter.7.cloned.1.call-done = bf16[128,1024]{1,0:T(8,128)(2,1)} async-done(((bf16[512,1024]{1,0:T(8,128)(2,1)}), bf16[128,1024]{1,0:T(8,128)(2,1)}) %reduce-scatter.7.cloned.1.call-update) | async-done | bytes 262160
  882.0 2.8 convolution_convert_fusion.2
  (267 shorter events, 192.4 us)
Async XLA Ops:
  6.5 1.6 copy-start
  6.5 3.8 copy-start.3
  6.5 23.3 %all-gather.3.cloned.1.call-start = ((), (), s32[]{:S(2)}) async-start(), calls=%async_computation.2 | async-start | bytes 1310720 | tf_op jit(solution)/shard_map/all_gather | solution.py:29
  10.3 96.7 %all-gather.5.cloned.1.call-start = ((), (), s32[]{:S(2)}) async-start(), calls=%async_computation.3 | async-start | bytes 4718592 | tf_op jit(solution)/shard_map/all_gather | solution.py:32
  14.7 93.9 %copy-start.1 = (s32[1,40]{1,0:T(1,128)S(1)}, s32[1,40]{1,0:T(1,128)}, u32[]{:S(2)}) copy-start(s32[1,40]{1,0:T(1,128)} %param.25) | copy-start | bytes 484
  14.7 93.9 %copy-start.2 = (s32[1,40]{1,0:T(1,128)S(1)}, s32[1,40]{1,0:T(1,128)}, u32[]{:S(2)}) copy-start(s32[1,40]{1,0:T(1,128)} %param.26) | copy-start | bytes 484
  14.7 93.9 %copy-start.4 = (s32[1,40]{1,0:T(1,128)S(1)}, s32[1,40]{1,0:T(1,128)}, u32[]{:S(2)}) copy-start(s32[1,40]{1,0:T(1,128)} %param.24) | copy-start | bytes 484
  14.7 838.6 %reduce-scatter.9.cloned.1.call-start = ((), (), s32[]{:S(2)}) async-start(), calls=%async_computation.5 | async-start | bytes 163840
  602.3 278.5 %reduce-scatter.7.cloned.1.call-start = ((), (), s32[]{:S(2)}) async-start(), calls=%async_computation.4 | async-start | bytes 1310720
Sparse Core Ops, SparseCore 0:
  10.4 19.4 all-gather.2
  31.9 75.0 all-gather.4
  602.4 250.8 reduce-scatter.8
  855.8 24.8 reduce-scatter.6
where the time goes:
time: 901 us; the launch traced here: 891 us
  waiting for transfers between devices  367 us (41%)
  loops' own time  145 us (16%)
  other arithmetic  98.3 us (11%)
  matrix products  97.9 us (11%)
  local copies, waits for them, and re-layouts  89.5 us (10%)
  blocking collectives  81 us (9%)
  between operations  13.2 us (1%)
    unnamed x6, waiting for transfers between devices  274 us
    another operation x1, loops' own time, body(): highest, denom, total = lax.fori_loop(0, block_count[0], one_block, init)  145 us
    pmax x1, blocking collectives, body(): lax.pmax(highest.astype(jnp.bfloat16), 'dev').astype(highest.dtype)  81 us
    all_gather x1, waiting for transfers between devices, body(): keyval = lax.all_gather(own_kv, 'grp', axis=0, tiled=True)  77.1 us
    dot_general x23, matrix products, one_block(): jnp.einsum('hts,she->the', weight.astype(jnp.bfloat16), message, preferre...  50.2 us
    dynamic_update_slice x23, other arithmetic, one_block(): lax.dynamic_update_slice_in_dim(total, old_t * jnp.repeat(factor, head_di...  48.9 us
    dynamic_slice x46, local copies, waits for them, and re-layouts, one_block(): lax.dynamic_slice_in_dim(all_queries, start, tile_rows, 0)  41.6 us
    slice x23, local copies, waits for them, and re-layouts, one_block(): values = src_rows[:, width:].reshape(tile_rows, heads, head_dim)  40.7 us
  transfers between devices with their start and end apart: 4, of which 4 were waited for; matrix products, arithmetic and copies ran while one was open for 1% of the time, Pallas kernels for 0%

commit v1 on v0

v1 whole, which is shorter than its diff:
```python
import functools

import jax
import jax.numpy as jnp
from jax import lax
from jax.experimental import pallas as pl
from jax.experimental.pallas import tpu as pltpu
from jax.sharding import PartitionSpec as P

BF = jnp.bfloat16
F32 = jnp.float32
LOG2E = 1.4426950408889634
EMPTY = -1e30
LANES = 128
UNROLL = 4


def pair_diag(w):
    zero = jnp.zeros_like(w[:, 0::2])
    upper = jnp.concatenate([w[:, 0::2], zero], axis=3)
    lower = jnp.concatenate([zero, w[:, 1::2]], axis=3)
    return jnp.concatenate([upper, lower], axis=2)


def split3(x):
    hi = x.astype(BF)
    rest = x - hi.astype(F32)
    mid = rest.astype(BF)
    lo = (rest - mid.astype(F32)).astype(BF)
    return hi, mid, lo


def attend(
    owners,
    heads,
    tile,
    head_dim,
    info,
    b_src,
    b_dst,
    b_type,
    prior,
    src,
    hub,
    wq,
    wk,
    wv,
    watt,
    wmsg,
    *rest,
):
    outs = rest[:owners]
    w_both, keys, values_t, queries_t, acc, top, den, stats = rest[owners:]
    step = pl.program_id(0)
    count = info[0]
    groups = src.shape[0] // tile
    width = 2 * head_dim

    w_both[:, :width] = wk[...]
    w_both[:, width:] = wv[...]

    def project(g, _):
        rows = pl.ds(pl.multiple_of(g * tile, tile), tile)
        kv = jnp.dot(src[rows, :], w_both[...], preferred_element_type=F32)
        keys[g] = kv[:, :width].astype(BF)
        values_t[g] = kv[:, width:].T.astype(BF)
        return 0

    lax.fori_loop(0, groups, project, 0)

    def project_q(t, _):
        rows = pl.ds(pl.multiple_of(t * tile, tile), tile)
        q = jnp.dot(hub[rows, :], wq[...], preferred_element_type=F32)
        queries_t[t] = q.T.astype(BF)
        acc[t] = jnp.zeros((width, tile), F32)
        top[t] = jnp.full((2, tile), EMPTY, F32)
        den[t] = jnp.zeros((2, tile), F32)
        return 0

    lax.fori_loop(0, owners, project_q, 0)

    lane = lax.broadcasted_iota(jnp.int32, (tile, width), 1)
    first = lane < head_dim

    def some_blocks(c, _):
        done = []
        for u in range(UNROLL):
            j = c * UNROLL + u
            valid = j < count
            jj = jnp.where(valid, j, 0)
            s_tile, d_tile, rtype = b_src[0, jj], b_dst[0, jj], b_type[0, jj]
            key_rel = jnp.dot(keys[s_tile], watt[rtype, 0], preferred_element_type=F32).astype(BF)
            zero = jnp.zeros_like(key_rel)
            stacked = jnp.concatenate(
                [jnp.where(first, key_rel, zero), jnp.where(first, zero, key_rel)], axis=0
            )
            scores = jnp.dot(stacked, queries_t[d_tile], preferred_element_type=F32)
            message_t = jnp.dot(
                wmsg[rtype, 0], values_t[s_tile], preferred_element_type=F32
            ).astype(BF)
            tops, sums, parts = [], [], []
            for i in range(2):
                scale = prior[rtype, 2 * step + i] * (LOG2E / float(head_dim) ** 0.5)
                s = scores[i * tile : (i + 1) * tile, :] * scale
                m = jnp.max(s, axis=0, keepdims=True)
                p = jnp.exp2(s - m)
                sums.append(jnp.sum(p, axis=0, keepdims=True))
                tops.append(m)
                parts.append(
                    jnp.dot(
                        message_t[i * head_dim : (i + 1) * head_dim, :],
                        p.astype(BF),
                        preferred_element_type=F32,
                    )
                )
            done.append((valid, d_tile, tops, sums, parts))
        for valid, d_tile, tops, sums, parts in done:
            for i in range(2):
                old = top[d_tile, i : i + 1, :]
                new = jnp.where(valid, jnp.maximum(old, tops[i]), old)
                keep = jnp.exp2(old - new)
                take = jnp.where(valid, jnp.exp2(tops[i] - new), 0.0)
                top[d_tile, i : i + 1, :] = new
                den[d_tile, i : i + 1, :] = den[d_tile, i : i + 1, :] * keep + sums[i] * take
                rows = pl.ds(i * head_dim, head_dim)
                acc[d_tile, rows, :] = acc[d_tile, rows, :] * keep + parts[i] * take
        return 0

    lax.fori_loop(0, (count + UNROLL - 1) // UNROLL, some_blocks, 0)

    for t in range(owners):
        for i in range(2):
            total = den[t, i : i + 1, :]
            some = total > 0.0
            safe = jnp.where(some, total, 1.0)
            lse = jnp.where(some, top[t, i : i + 1, :] + jnp.log(safe) * LOG2E, EMPTY)
            stats[t, pl.ds(2 * step + i, 1), :] = lse
            rows = pl.ds(pl.multiple_of((2 * step + i) * head_dim, head_dim), head_dim)
            outs[t][rows, :] = (acc[t, pl.ds(i * head_dim, head_dim), :] * (1.0 / safe)).astype(BF)

    @pl.when(step == pl.num_programs(0) - 1)
    def _():
        for t in range(owners):
            parts = split3(stats[t])
            for k in range(3):
                outs[t][pl.ds(heads * head_dim + k * heads, heads), :] = parts[k]


def combine(owners, heads, head_dim, *refs):
    parts, w_out, out, agg = refs[:owners], refs[owners], refs[owners + 1], refs[owners + 2]
    base = heads * head_dim
    lse = []
    for r in parts:
        hi, mid, lo = (
            r[pl.ds(base + k * heads, heads), :].astype(F32) for k in range(3)
        )
        lse.append((hi + mid) + lo)
    best = functools.reduce(jnp.maximum, lse)
    weights = [jnp.exp2(v - best) for v in lse]
    whole = functools.reduce(jnp.add, weights)
    weights = [w / whole for w in weights]
    for h in range(heads):
        rows = pl.ds(h * head_dim, head_dim)
        total = functools.reduce(
            jnp.add,
            [r[rows, :].astype(F32) * w[h : h + 1, :] for r, w in zip(parts, weights)],
        )
        agg[:, h * head_dim : (h + 1) * head_dim] = total.T.astype(BF)
    out[...] = jnp.dot(agg[...], w_out[...], preferred_element_type=F32).astype(BF)


def body(
    node_src,
    hub_feat,
    w_query,
    w_key,
    w_value,
    w_out,
    w_att,
    w_msg,
    relation_prior,
    block_src,
    block_dst,
    block_type,
    block_count,
):
    groups = lax.axis_size("grp")
    owners = lax.axis_size("dev")
    tile, width = hub_feat.shape
    relations, heads = relation_prior.shape
    head_dim = width // heads
    pair = 2 * head_dim
    slots = block_src.shape[1]
    my_grp = lax.axis_index("grp")
    my_dev = lax.axis_index("dev")

    all_src = [node_src]
    all_hub = [hub_feat]
    for k in range(1, owners):
        all_hub.append(lax.ppermute(hub_feat, "dev", [(i, i ^ k) for i in range(owners)]))
    swap = [(i, i ^ 1) for i in range(groups)]
    all_src = {0: node_src, 1: lax.ppermute(node_src, "grp", swap)}
    order = [2, 6, 4] if groups == 8 else list(range(2, groups, 2))
    for k in order:
        all_src[k] = lax.ppermute(node_src, "grp", [(i, i ^ k) for i in range(groups)])
    for k in order:
        all_src[k + 1] = lax.ppermute(all_src[k], "grp", swap)
    src = jnp.concatenate([all_src[k] for k in range(groups)], axis=0)
    hub = jnp.concatenate(all_hub, axis=0)

    att = pair_diag(w_att)
    msg = pair_diag(jnp.swapaxes(w_msg, 2, 3))
    rows_out = width + 3 * heads
    whole = lambda shape: pl.BlockSpec(shape, lambda h, *_: (0,) * len(shape))
    column = pl.BlockSpec((width, pair), lambda h, *_: (0, h))
    maps = pl.BlockSpec((relations, 1, pair, pair), lambda h, *_: (0, h, 0, 0))
    blocks = slots * heads
    tiles = pl.pallas_call(
        functools.partial(attend, owners, heads, tile, head_dim),
        grid_spec=pltpu.PrefetchScalarGridSpec(
            num_scalar_prefetch=5,
            grid=(heads // 2,),
            in_specs=[whole(src.shape), whole(hub.shape), column, column, column, maps, maps],
            out_specs=[whole((rows_out, tile))] * owners,
            scratch_shapes=[
                pltpu.VMEM((width, 2 * pair), BF),
                pltpu.VMEM((groups, tile, pair), BF),
                pltpu.VMEM((groups, pair, tile), BF),
                pltpu.VMEM((owners, pair, tile), BF),
                pltpu.VMEM((owners, pair, tile), F32),
                pltpu.VMEM((owners, 2, tile), F32),
                pltpu.VMEM((owners, 2, tile), F32),
                pltpu.VMEM((owners, heads, tile), F32),
            ],
        ),
        out_shape=[jax.ShapeDtypeStruct((rows_out, tile), BF)] * owners,
        cost_estimate=pl.CostEstimate(
            flops=blocks * tile * tile * head_dim * 8, bytes_accessed=1 << 24, transcendentals=0
        ),
        name="attend",
    )(
        block_count,
        block_src ^ my_grp,
        block_dst ^ my_dev,
        block_type,
        relation_prior,
        src,
        hub,
        w_query,
        w_key,
        w_value,
        att,
        msg,
    )
    parts = [tiles[0]]
    for k in range(1, owners):
        parts.append(lax.ppermute(tiles[k], "dev", [(i, i ^ k) for i in range(owners)]))
    return pl.pallas_call(
        functools.partial(combine, owners, heads, head_dim),
        out_shape=jax.ShapeDtypeStruct((tile, width), BF),
        scratch_shapes=[pltpu.VMEM((tile, width), BF)],
        name="combine",
    )(*parts, w_out)


def solution(mesh):
    rows = P(("grp", "dev"), None)
    placed = (rows, rows) + (P(),) * 7 + (rows,) * 3 + (P(("grp", "dev")),)
    return jax.shard_map(body, mesh=mesh, in_specs=placed, out_specs=rows, check_vma=False)
```

time: 901 us -> 208 us (0.23)
  the two profiles are of different devices: /device:TPU:0 before, /device:TPU:29 now
where the time goes in v1:
time: 208 us
  Pallas kernels  147 us (71%)
  waiting for transfers between devices  28.2 us (14%)
  local copies, waits for them, and re-layouts  13.5 us (6%)
  starting transfers between devices  12.2 us (6%)
  other arithmetic  6.26 us (3%)
    pallas_call x1, Pallas kernels, body(): pl.pallas_call(functools.partial(attend, owners, heads, tile, head_dim),...  143 us
    ppermute x3, waiting for transfers between devices, body(): lax.ppermute(tiles[k], 'dev', [(i, i ^ k) for i in range(owners)])  12.3 us
    ppermute x3, waiting for transfers between devices, body(): lax.ppermute(hub_feat, 'dev', [(i, i ^ k) for i in range(owners)])  9.14 us
    unnamed x26, local copies, waits for them, and re-layouts  8.73 us
    ppermute x3, waiting for transfers between devices, body(): all_src[k + 1] = lax.ppermute(all_src[k], 'grp', swap)  6.76 us
    slice x2, local copies, waits for them, and re-layouts, pair_diag(): upper = jnp.concatenate([w[:, 0::2], zero], axis=3)  4.77 us
    concatenate x1, other arithmetic, pair_diag(): return jnp.concatenate([upper, lower], axis=2)  4.63 us
  transfers between devices with their start and end apart: 13, of which 6 were waited for; matrix products, arithmetic and copies ran while one was open for 8% of the time, Pallas kernels for 0%

profile of v1, /device:TPU:29, one launch (start us, length us, event | category | flops | bytes accessed | tf_op | source)
XLA Modules:
  0.0 207.6 jit_solution(16094093359244706184)
XLA Ops:
  0.0 0.2 collective-permute-start.1
  0.2 1.2 collective-permute-start
  1.4 0.1 collective-permute-start.3
  1.4 3.3 %collective-permute-start.5 = (bf16[128,1024]{1,0:T(8,128)(2,1)}, bf16[128,1024]{1,0:T(8,128)(2,1)S(1)}, u32[]{:S(2)}, u32[]{:S(2)}) collective-permute-start(bf16[128,1024]{1,0:T(8,128)(2,1)} %param.13), channel_id=1, source_target_pairs={{0,24},{4,28},{8,16},{12,20},{16,8},{20,12},{24,0},{28,4},{1,25},{... | collective-permute-start | bytes 786440 | tf_op jit(solution)/shard_map/ppermute | solution.py:205
  4.8 1.8 collective-permute-start.7
  6.6 6.4 %copy.14 = bf16[16,16,64,64]{2,3,1,0:T(8,128)(2,1)} copy(bf16[16,16,64,64]{3,2,1,0:T(8,128)(2,1)} %param.20) | data formatting | bytes 4194304 | tf_op args[7]
  12.9 3.4 %fusion.6 = (bf16[16,8,64,64]{3,2,1,0:T(8,128)(2,1)S(1)}, bf16[16,8,64,64]{3,2,1,0:T(8,128)(2,1)S(1)}) fusion(bf16[16,16,64,64]{3,2,1,0:T(8,128)(2,1)} %bitcast.1), kind=kLoop, calls=%fused_computation.19 | loop fusion | bytes 4194304 | tf_op jit(solution)/shard_map/slice | solution.py:20
  16.3 0.1 copy-done
  16.4 1.4 fusion.7
  17.8 0.0 copy-start.5
  17.8 0.0 copy-start.7
  17.8 0.0 copy-start.8
  17.8 0.0 copy-start.4
  17.9 4.6 %fusion.4 = (bf16[16,8,128,128]{3,2,1,0:T(8,128)(2,1)}, bf16[16,8,128,128]{3,2,1,0:T(8,128)(2,1)}) fusion(bf16[16,8,64,64]{3,2,1,0:T(8,128)(2,1)S(1)} %get-tuple-element.16, bf16[16,8,64,64]{3,2,1,0:T(8,128)(2,1)S(1)} %get-tuple-element.15, bf16[16,8,64,64]{3,2,1,0:T(8,128)(2,1)S(1)} %get-tuple-element.14, bf16[16,8,64,64]{3,2,1,0:T(8,128)(2,1)S(1)} %get-tuple-element.13), kind=kLoop, calls=%fused_computation.6 | loop fusion | flops 29360128 | bytes 12582912 | tf_op jit(solution)/shard_map/concatenate | solution.py:22
  22.5 0.0 collective-permute-done.1
  22.5 0.0 copy-done.5
  22.5 0.2 collective-permute-start.8
  22.7 0.0 collective-permute-done
  22.7 1.4 collective-permute-start.9
  24.1 0.0 copy-done.7
  24.1 0.0 copy-done.8
  24.1 0.6 broadcast_xor_fusion
  25.4 0.0 copy-done.4
  25.4 0.0 collective-permute-done.3
  25.4 0.3 collective-permute-start.2
  25.8 0.0 collective-permute-done.5
  25.8 1.3 collective-permute-start.4
  27.0 0.0 collective-permute-done.7
  27.0 0.3 collective-permute-start.6
  27.3 3.1 %collective-permute-done.8 = bf16[128,1024]{1,0:T(8,128)(2,1)S(1)} collective-permute-done((bf16[128,1024]{1,0:T(8,128)(2,1)S(1)}, bf16[128,1024]{1,0:T(8,128)(2,1)S(1)}, u32[]{:S(2)}, u32[]{:S(2)}) %collective-permute-start.8) | collective-permute-done | bytes 262176 | tf_op jit(solution)/shard_map/ppermute | solution.py:200
  30.4 6.0 %collective-permute-done.9 = bf16[128,1024]{1,0:T(8,128)(2,1)S(1)} collective-permute-done((bf16[128,1024]{1,0:T(8,128)(2,1)S(1)}, bf16[128,1024]{1,0:T(8,128)(2,1)S(1)}, u32[]{:S(2)}, u32[]{:S(2)}) %collective-permute-start.9) | collective-permute-done | bytes 262176 | tf_op jit(solution)/shard_map/ppermute | solution.py:200
  36.4 1.1 pad_maximum_fusion.hub
  37.5 0.0 collective-permute-done.2
  37.6 1.2 collective-permute-done.4
  38.8 5.6 %collective-permute-done.6 = bf16[128,1024]{1,0:T(8,128)(2,1)S(1)} collective-permute-done((bf16[128,1024]{1,0:T(8,128)(2,1)S(1)}, bf16[128,1024]{1,0:T(8,128)(2,1)S(1)}, u32[]{:S(2)}, u32[]{:S(2)}) %collective-permute-start.6) | collective-permute-done | bytes 262176 | tf_op jit(solution)/shard_map/ppermute | solution.py:207
  44.4 0.0 copy-start.6
  44.4 1.4 copy-done.6
  45.8 143.1 %attend.1 = (bf16[1072,128]{1,0:T(8,128)(2,1)}, bf16[1072,128]{1,0:T(8,128)(2,1)}, bf16[1072,128]{1,0:T(8,128)(2,1)}, bf16[1072,128]{1,0:T(8,128)(2,1)}) custom-call(s32[1]{0:T(128)S(6)} %copy.22.info, s32[1,40]{1,0:T(1,128)} %get-tuple-element.20.b_src, s32[1,40]{1,0:T(1,128)} %get-tuple-element.19.b_dst, s32[1,40]{1,0:T(1,128)} %b_type.1, f32[16,16]{1,0:T(8,128)} %prior.1, ...), custom_call_target="tpu_custom_call" | custom-call | flops 5368709120 | bytes 16777216 | tf_op jit(solution)/shard_map/attend/pallas_call | solution.py:218
  188.9 0.0 collective-permute-start.10
  188.9 0.1 collective-permute-start.11
  189.0 2.1 collective-permute-start.12
  191.0 0.0 collective-permute-done.10.refs_1_
  191.0 5.8 %collective-permute-done.11.refs_2_ = bf16[1072,128]{1,0:T(8,128)(2,1)S(1)} collective-permute-done((bf16[1072,128]{1,0:T(8,128)(2,1)}, bf16[1072,128]{1,0:T(8,128)(2,1)S(1)}, u32[]{:S(2)}, u32[]{:S(2)}) %collective-permute-start.11) | collective-permute-done | bytes 274464 | tf_op jit(solution)/shard_map/ppermute | solution.py:257
  196.9 6.5 %collective-permute-done.12.refs_3_ = bf16[1072,128]{1,0:T(8,128)(2,1)S(1)} collective-permute-done((bf16[1072,128]{1,0:T(8,128)(2,1)}, bf16[1072,128]{1,0:T(8,128)(2,1)S(1)}, u32[]{:S(2)}, u32[]{:S(2)}) %collective-permute-start.12) | collective-permute-done | bytes 274464 | tf_op jit(solution)/shard_map/ppermute | solution.py:257
  203.3 0.0 copy-done.1
  203.3 0.0 copy-done.2
  203.3 0.7 copy-done.3
  204.0 3.5 %combine.1 = bf16[128,1024]{1,0:T(8,128)(2,1)} custom-call(bf16[1072,128]{1,0:T(8,128)(2,1)} %get-tuple-element.9.refs_0_, bf16[1072,128]{1,0:T(8,128)(2,1)} %copy-done.1, bf16[1072,128]{1,0:T(8,128)(2,1)} %copy-done.2, bf16[1072,128]{1,0:T(8,128)(2,1)} %copy-done.3, bf16[1024,1024]{1,0:T(8,128)(2,1)} %refs_4_.1), custom_call_target="tpu_custom_call" | custom-call | tf_op jit(solution)/shard_map/combine/pallas_call | solution.py:258
  (12 shorter events, 0.2 us)
Async XLA Ops:
  0.0 22.5 %collective-permute-start.1 = (bf16[128,1024]{1,0:T(8,128)(2,1)}, bf16[128,1024]{1,0:T(8,128)(2,1)S(1)}, u32[]{:S(2)}, u32[]{:S(2)}) collective-permute-start(bf16[128,1024]{1,0:T(8,128)(2,1)} %param.13), channel_id=1, source_target_pairs={{0,8},{4,12},{8,0},{12,4},{16,24},{20,28},{24,16},{28,20},{1,9},{5... | collective-permute-start | bytes 786440 | tf_op jit(solution)/shard_map/ppermute | solution.py:205
  0.2 22.6 %collective-permute-start = (bf16[128,1024]{1,0:T(8,128)(2,1)}, bf16[128,1024]{1,0:T(8,128)(2,1)S(1)}, u32[]{:S(2)}, u32[]{:S(2)}) collective-permute-start(bf16[128,1024]{1,0:T(8,128)(2,1)} %param.13), channel_id=1, source_target_pairs={{0,4},{4,0},{8,12},{12,8},{16,20},{20,16},{24,28},{28,24},{1,5},{5... | collective-permute-start | bytes 786440 | tf_op jit(solution)/shard_map/ppermute | solution.py:202
  1.4 24.0 %collective-permute-start.3 = (bf16[128,1024]{1,0:T(8,128)(2,1)}, bf16[128,1024]{1,0:T(8,128)(2,1)S(1)}, u32[]{:S(2)}, u32[]{:S(2)}) collective-permute-start(bf16[128,1024]{1,0:T(8,128)(2,1)} %param.13), channel_id=1, source_target_pairs={{0,16},{4,20},{8,24},{12,28},{16,0},{20,4},{24,8},{28,12},{1,17},{... | collective-permute-start | bytes 786440 | tf_op jit(solution)/shard_map/ppermute | solution.py:205
  1.4 24.3 %collective-permute-start.5 = (bf16[128,1024]{1,0:T(8,128)(2,1)}, bf16[128,1024]{1,0:T(8,128)(2,1)S(1)}, u32[]{:S(2)}, u32[]{:S(2)}) collective-permute-start(bf16[128,1024]{1,0:T(8,128)(2,1)} %param.13), channel_id=1, source_target_pairs={{0,24},{4,28},{8,16},{12,20},{16,8},{20,12},{24,0},{28,4},{1,25},{... | collective-permute-start | bytes 786440 | tf_op jit(solution)/shard_map/ppermute | solution.py:205
  4.8 22.3 %collective-permute-start.7 = (bf16[128,1024]{1,0:T(8,128)(2,1)}, bf16[128,1024]{1,0:T(8,128)(2,1)S(1)}, u32[]{:S(2)}, u32[]{:S(2)}) collective-permute-start(bf16[128,1024]{1,0:T(8,128)(2,1)} %param.14), channel_id=1, source_target_pairs={{0,1},{1,0},{2,3},{3,2},{4,5},{5,4},{6,7},{7,6},{8,9},{9,8},{10,11... | collective-permute-start | bytes 786440 | tf_op jit(solution)/shard_map/ppermute | solution.py:200
  12.9 3.5 %copy-start = (bf16[16,16,64,64]{3,2,1,0:T(8,128)(2,1)S(1)}, bf16[16,16,64,64]{3,2,1,0:T(8,128)(2,1)}, u32[]{:S(2)}) copy-start(bf16[16,16,64,64]{3,2,1,0:T(8,128)(2,1)} %param.19) | copy-start | bytes 6291460
  17.8 4.7 %copy-start.5 = (bf16[128,1024]{1,0:T(8,128)(2,1)S(1)}, bf16[128,1024]{1,0:T(8,128)(2,1)}, u32[]{:S(2)}) copy-start(bf16[128,1024]{1,0:T(8,128)(2,1)} %param.14) | copy-start | bytes 786436
  17.8 6.3 %copy-start.7 = (s32[1,40]{1,0:T(1,128)S(1)}, s32[1,40]{1,0:T(1,128)}, u32[]{:S(2)}) copy-start(s32[1,40]{1,0:T(1,128)} %param.23) | copy-start | bytes 484
  17.8 6.3 %copy-start.8 = (s32[1,40]{1,0:T(1,128)S(1)}, s32[1,40]{1,0:T(1,128)}, u32[]{:S(2)}) copy-start(s32[1,40]{1,0:T(1,128)} %param.22) | copy-start | bytes 484
  17.8 7.5 %copy-start.4 = (bf16[128,1024]{1,0:T(8,128)(2,1)S(1)}, bf16[128,1024]{1,0:T(8,128)(2,1)}, u32[]{:S(2)}) copy-start(bf16[128,1024]{1,0:T(8,128)(2,1)} %param.13) | copy-start | bytes 786436
  22.5 7.9 %collective-permute-start.8 = (bf16[128,1024]{1,0:T(8,128)(2,1)S(1)}, bf16[128,1024]{1,0:T(8,128)(2,1)S(1)}, u32[]{:S(2)}, u32[]{:S(2)}) collective-permute-start(bf16[128,1024]{1,0:T(8,128)(2,1)S(1)} %copy-done.5), channel_id=1, source_target_pairs={{0,2},{1,3},{2,0},{3,1},{4,6},{5,7},{6,4},{7,5},{8,10},{9,11},{10,... | collective-permute-start | bytes 786440 | tf_op jit(solution)/shard_map/ppermute | solution.py:200
  22.7 13.7 %collective-permute-start.9 = (bf16[128,1024]{1,0:T(8,128)(2,1)S(1)}, bf16[128,1024]{1,0:T(8,128)(2,1)S(1)}, u32[]{:S(2)}, u32[]{:S(2)}) collective-permute-start(bf16[128,1024]{1,0:T(8,128)(2,1)S(1)} %copy-done.5), channel_id=1, source_target_pairs={{0,3},{1,2},{2,1},{3,0},{4,7},{5,6},{6,5},{7,4},{8,11},{9,10},{10,... | collective-permute-start | bytes 786440 | tf_op jit(solution)/shard_map/ppermute | solution.py:200
  25.4 12.1 %collective-permute-start.2 = (bf16[128,1024]{1,0:T(8,128)(2,1)S(1)}, bf16[128,1024]{1,0:T(8,128)(2,1)S(1)}, u32[]{:S(2)}, u32[]{:S(2)}) collective-permute-start(bf16[128,1024]{1,0:T(8,128)(2,1)S(1)} %collective-permute-done.1), channel_id=1, source_target_pairs={{0,4},{4,0},{8,12},{12,8},{16,20},{20,16},{24,28},{28,24},{1,5},{5... | collective-permute-start | bytes 786440 | tf_op jit(solution)/shard_map/ppermute | solution.py:207
  25.8 13.0 %collective-permute-start.4 = (bf16[128,1024]{1,0:T(8,128)(2,1)S(1)}, bf16[128,1024]{1,0:T(8,128)(2,1)S(1)}, u32[]{:S(2)}, u32[]{:S(2)}) collective-permute-start(bf16[128,1024]{1,0:T(8,128)(2,1)S(1)} %collective-permute-done.3), channel_id=1, source_target_pairs={{0,4},{4,0},{8,12},{12,8},{16,20},{20,16},{24,28},{28,24},{1,5},{5... | collective-permute-start | bytes 786440 | tf_op jit(solution)/shard_map/ppermute | solution.py:207
  27.0 17.3 %collective-permute-start.6 = (bf16[128,1024]{1,0:T(8,128)(2,1)S(1)}, bf16[128,1024]{1,0:T(8,128)(2,1)S(1)}, u32[]{:S(2)}, u32[]{:S(2)}) collective-permute-start(bf16[128,1024]{1,0:T(8,128)(2,1)S(1)} %collective-permute-done.5), channel_id=1, source_target_pairs={{0,4},{4,0},{8,12},{12,8},{16,20},{20,16},{24,28},{28,24},{1,5},{5... | collective-permute-start | bytes 786440 | tf_op jit(solution)/shard_map/ppermute | solution.py:207
  44.4 1.4 copy-start.6
  188.9 2.1 %collective-permute-start.10 = (bf16[1072,128]{1,0:T(8,128)(2,1)}, bf16[1072,128]{1,0:T(8,128)(2,1)S(1)}, u32[]{:S(2)}, u32[]{:S(2)}) collective-permute-start(bf16[1072,128]{1,0:T(8,128)(2,1)} %get-tuple-element.10), channel_id=1, source_target_pairs={{0,1},{1,0},{2,3},{3,2},{4,5},{5,4},{6,7},{7,6},{8,9},{9,8},{10,11... | collective-permute-start | bytes 823304 | tf_op jit(solution)/shard_map/ppermute | solution.py:257
  188.9 8.0 %collective-permute-start.11 = (bf16[1072,128]{1,0:T(8,128)(2,1)}, bf16[1072,128]{1,0:T(8,128)(2,1)S(1)}, u32[]{:S(2)}, u32[]{:S(2)}) collective-permute-start(bf16[1072,128]{1,0:T(8,128)(2,1)} %get-tuple-element.11), channel_id=1, source_target_pairs={{0,2},{1,3},{2,0},{3,1},{4,6},{5,7},{6,4},{7,5},{8,10},{9,11},{10,... | collective-permute-start | bytes 823304 | tf_op jit(solution)/shard_map/ppermute | solution.py:257
  189.0 14.4 %collective-permute-start.12 = (bf16[1072,128]{1,0:T(8,128)(2,1)}, bf16[1072,128]{1,0:T(8,128)(2,1)S(1)}, u32[]{:S(2)}, u32[]{:S(2)}) collective-permute-start(bf16[1072,128]{1,0:T(8,128)(2,1)} %get-tuple-element.12), channel_id=1, source_target_pairs={{0,3},{1,2},{2,1},{3,0},{4,7},{5,6},{6,5},{7,4},{8,11},{9,10},{10,... | collective-permute-start | bytes 823304 | tf_op jit(solution)/shard_map/ppermute | solution.py:257
  191.0 12.3 %copy-start.1 = (bf16[1072,128]{1,0:T(8,128)(2,1)}, bf16[1072,128]{1,0:T(8,128)(2,1)S(1)}, u32[]{:S(2)}) copy-start(bf16[1072,128]{1,0:T(8,128)(2,1)S(1)} %collective-permute-done.10.refs_1_) | copy-start | bytes 823300
  196.9 6.5 %copy-start.2 = (bf16[1072,128]{1,0:T(8,128)(2,1)}, bf16[1072,128]{1,0:T(8,128)(2,1)S(1)}, u32[]{:S(2)}) copy-start(bf16[1072,128]{1,0:T(8,128)(2,1)S(1)} %collective-permute-done.11.refs_2_) | copy-start | bytes 823300
  203.3 0.7 copy-start.3

commit v2 on v0

v2 whole, which is shorter than its diff:
```python
import functools

import jax
import jax.numpy as jnp
from jax import lax
from jax.experimental import pallas as pl
from jax.experimental.pallas import tpu as pltpu
from jax.sharding import PartitionSpec as P

BF = jnp.bfloat16
F32 = jnp.float32
LOG2E = 1.4426950408889634
EMPTY = -1e30
BLOCKS = 2
LAGS = (4, 8, 12)
LIMIT = 16 << 20


def split3(x):
    hi = x.astype(BF)
    rest = x - hi.astype(F32)
    mid = rest.astype(BF)
    lo = (rest - mid.astype(F32)).astype(BF)
    return hi, mid, lo


def prepare(att, msg, att_out, msg_out):
    kinds, pairs, pair, head_dim = att.shape
    row = lax.broadcasted_iota(jnp.int32, (pair, head_dim), 0)
    col = lax.broadcasted_iota(jnp.int32, (pair, head_dim), 1)
    twice = jnp.where((row & (head_dim - 1)) == col, 1.0, 0.0).astype(BF)
    r2 = lax.broadcasted_iota(jnp.int32, (pair, pair), 0)
    c2 = lax.broadcasted_iota(jnp.int32, (pair, pair), 1)
    same = (r2 < head_dim) == (c2 < head_dim)
    dims = (((1,), (1,)), ((), ()))
    for r in range(kinds):
        for h in range(pairs):
            a = lax.dot_general(att[r, h], twice, dims, preferred_element_type=F32)
            att_out[r, h] = jnp.where(same, a, 0.0).astype(BF)
            m = lax.dot_general(twice, msg[r, h], dims, preferred_element_type=F32)
            msg_out[r, h] = jnp.where(same, m, 0.0).astype(BF)


def run_blocks(
    owners, heads, tile, head_dim, slots, count, b_src, b_dst, b_type, prior, tiles, wk, wv, att, msg,
    queries, acc, top, den, order, src, keys, values,
):
    width = heads * head_dim
    pair, quad = 2 * head_dim, 4 * head_dim
    quads = heads // 4
    for i, ref in enumerate(tiles):
        src[i * tile : (i + 1) * tile, :] = ref[...]
    for q in range(quads):
        cols = slice(q * quad, (q + 1) * quad)
        k = jnp.dot(src[...], wk[:, cols], preferred_element_type=F32)
        v = jnp.dot(src[...], wv[:, cols], preferred_element_type=F32)
        for i in range(len(slots)):
            rows = slice(i * tile, (i + 1) * tile)
            keys[i, q] = k[rows, :].astype(BF)
            values[i, q] = v[rows, :].T.astype(BF)

    def pick(j, n):
        s = b_src[0, j]
        which = jnp.int32(0)
        hit = s == slots[0]
        for i in range(1, len(slots)):
            here = s == slots[i]
            which = jnp.where(here, i, which)
            hit = hit | here
        order[0, n] = j
        order[1, n] = which
        return n + hit.astype(jnp.int32)

    total = lax.fori_loop(0, count[0], pick, jnp.int32(0))
    lane = lax.broadcasted_iota(jnp.int32, (tile, pair), 1)
    left = lane < head_dim
    none = jnp.zeros((pair, pair), BF)

    def diag(w, r, q):
        upper = jnp.concatenate([w[r, 2 * q], none], axis=1)
        lower = jnp.concatenate([none, w[r, 2 * q + 1]], axis=1)
        return jnp.concatenate([upper, lower], axis=0)

    def some_blocks(c, _):
        blocks = []
        for u in range(BLOCKS):
            n = c * BLOCKS + u
            valid = n < total
            j = jnp.where(valid, order[0, n], 0)
            s = jnp.where(valid, order[1, n], 0)
            blocks.append((valid, s, b_dst[0, j], b_type[0, j]))

        def maps(u, q):
            _, s, _, r = blocks[u]
            key_rel = jnp.dot(keys[s, q], diag(att, r, q), preferred_element_type=F32).astype(BF)
            message = jnp.dot(diag(msg, r, q), values[s, q], preferred_element_type=F32).astype(BF)
            return key_rel, message

        def scores(u, h, key_rel):
            _, _, d, _ = blocks[u]
            k = key_rel[:, (h % 2) * pair : (h % 2 + 1) * pair]
            zero = jnp.zeros_like(k)
            both = jnp.concatenate([jnp.where(left, k, zero), jnp.where(left, zero, k)], axis=0)
            q = queries[d, h * pair : (h + 1) * pair, :]
            return jnp.dot(both, q, preferred_element_type=F32)

        def weigh(u, h, s):
            _, _, _, r = blocks[u]
            found = []
            for i in range(2):
                scale = prior[r, 2 * h + i] * (LOG2E / float(head_dim) ** 0.5)
                x = s[i * tile : (i + 1) * tile, :] * scale
                m = jnp.max(x, axis=0, keepdims=True)
                p = jnp.exp2(x - m)
                found.append((m, jnp.sum(p, axis=0, keepdims=True), p.astype(BF)))
            return found

        def gather(u, h, message, found):
            valid, _, d, _ = blocks[u]
            for i in range(2):
                row = (h % 2) * pair + i * head_dim
                m, total_w, p = found[i]
                part = jnp.dot(message[row : row + head_dim, :], p, preferred_element_type=F32)
                head = 2 * h + i
                one = slice(head, head + 1)
                rows = slice(head * head_dim, (head + 1) * head_dim)
                old = top[d, one, :]
                new = jnp.where(valid, jnp.maximum(old, m), old)
                keep = jnp.exp2(old - new)
                add = jnp.where(valid, jnp.exp2(m - new), 0.0)
                top[d, one, :] = new
                den[d, one, :] = den[d, one, :] * keep + total_w * add
                acc[d, rows, :] = acc[d, rows, :] * keep + part * add

        items = [(u, h) for u in range(BLOCKS) for h in range(heads // 2)]
        mapped, scored, weighed = {}, {}, {}
        a, b, d = LAGS
        for t in range(len(items) + d):
            if t < len(items) and items[t][1] % 2 == 0:
                u, h = items[t]
                mapped[u, h // 2] = maps(u, h // 2)
            if 0 <= t - a < len(items):
                u, h = items[t - a]
                scored[u, h] = scores(u, h, mapped[u, h // 2][0])
            if 0 <= t - b < len(items):
                u, h = items[t - b]
                weighed[u, h] = weigh(u, h, scored.pop((u, h)))
            if 0 <= t - d < len(items):
                u, h = items[t - d]
                gather(u, h, mapped[u, h // 2][1], weighed.pop((u, h)))
        return 0

    lax.fori_loop(0, (total + BLOCKS - 1) // BLOCKS, some_blocks, 0)


def first_phase(shape, slots, *refs):
    owners, heads, tile, head_dim = shape
    n = len(slots)
    count, b_src, b_dst, b_type, prior = refs[:5]
    tiles = refs[5 : 5 + n]
    wk, wv, att, msg, wq = refs[5 + n : 10 + n]
    hubs = refs[10 + n : 10 + n + owners]
    queries, acc, top, den, order, src, keys, values = refs[10 + n + owners :]
    quad = 4 * head_dim
    acc[...] = jnp.zeros(acc.shape, F32)
    top[...] = jnp.full(top.shape, EMPTY, F32)
    den[...] = jnp.zeros(den.shape, F32)
    for lo in range(0, owners, n):
        some = range(lo, min(lo + n, owners))
        for i, t in enumerate(some):
            src[i * tile : (i + 1) * tile, :] = hubs[t][...]
        for c in range(0, heads * head_dim, quad):
            q = jnp.dot(src[...], wq[:, c : c + quad], preferred_element_type=F32)
            for i, t in enumerate(some):
                queries[t, c : c + quad, :] = q[i * tile : (i + 1) * tile, :].T.astype(BF)
    run_blocks(
        *shape, slots, count, b_src, b_dst, b_type, prior, tiles, wk, wv, att, msg,
        queries, acc, top, den, order, src, keys, values,
    )


def later_phase(shape, slots, last, *refs):
    owners, heads, tile, head_dim = shape
    n = len(slots)
    count, b_src, b_dst, b_type, prior = refs[:5]
    tiles = refs[5 : 5 + n]
    wk, wv, att, msg, queries = refs[5 + n : 10 + n]
    given = refs[10 + n : 13 + n]
    rest = refs[13 + n :]
    if last:
        outs, rest = rest[:owners], rest[owners:]
        order, src, keys, values = rest
        acc, top, den = given
    else:
        acc, top, den, order, src, keys, values = rest
        acc[...], top[...], den[...] = (g[...] for g in given)
    run_blocks(
        *shape, slots, count, b_src, b_dst, b_type, prior, tiles, wk, wv, att, msg,
        queries, acc, top, den, order, src, keys, values,
    )
    if last:
        for t in range(owners):
            total = den[t]
            some = total > 0.0
            safe = jnp.where(some, total, 1.0)
            lse = jnp.where(some, top[t] + jnp.log(safe) * LOG2E, EMPTY)
            inverse = 1.0 / safe
            for h in range(heads):
                rows = slice(h * head_dim, (h + 1) * head_dim)
                outs[t][rows, :] = (acc[t, rows, :] * inverse[h : h + 1, :]).astype(BF)
            parts = split3(lse)
            for k in range(3):
                base = heads * head_dim + k * heads
                outs[t][base : base + heads, :] = parts[k]


def combine(owners, heads, head_dim, *refs):
    parts, w_out, out, agg = refs[:owners], refs[owners], refs[owners + 1], refs[owners + 2]
    base = heads * head_dim
    lse = []
    for r in parts:
        hi, mid, lo = (r[base + k * heads : base + (k + 1) * heads, :].astype(F32) for k in range(3))
        lse.append((hi + mid) + lo)
    best = functools.reduce(jnp.maximum, lse)
    weights = [jnp.exp2(v - best) for v in lse]
    whole = functools.reduce(jnp.add, weights)
    weights = [w / whole for w in weights]
    for h in range(heads):
        rows = slice(h * head_dim, (h + 1) * head_dim)
        total = functools.reduce(
            jnp.add,
            [r[rows, :].astype(F32) * w[h : h + 1, :] for r, w in zip(parts, weights)],
        )
        agg[:, rows] = total.T.astype(BF)
    out[...] = jnp.dot(agg[...], w_out[...], preferred_element_type=F32).astype(BF)


def body(
    node_src,
    hub_feat,
    w_query,
    w_key,
    w_value,
    w_out,
    w_att,
    w_msg,
    relation_prior,
    block_src,
    block_dst,
    block_type,
    block_count,
):
    groups = lax.axis_size("grp")
    owners = lax.axis_size("dev")
    tile, width = hub_feat.shape
    relations, heads = relation_prior.shape
    head_dim = width // heads
    pair, pairs = 2 * head_dim, heads // 2
    quads = heads // 4
    length = block_src.shape[1]
    shape = (owners, heads, tile, head_dim)
    smem = pl.BlockSpec(memory_space=pltpu.SMEM)
    keep = lambda x: pltpu.with_memory_space_constraint(x, pltpu.VMEM)
    w_query, w_key, w_value, w_out = (keep(w) for w in (w_query, w_key, w_value, w_out))
    vmem = pl.BlockSpec(memory_space=pltpu.VMEM)

    def move(x, axis, size, k):
        return lax.ppermute(x, axis, [(i, i ^ k) for i in range(size)])

    hubs = {0: hub_feat}
    for k in range(1, owners):
        far = k > 1 and k % 2 == 1
        hubs[k] = move(hubs[k - 1] if far else hub_feat, "dev", owners, 1 if far else k)
    srcs = {0: node_src}
    if groups == 8:
        steps = [(0, 1), (2, 3), (6, 4), (7, 5)]
        for k in (1, 2, 3, 6, 4):
            srcs[k] = move(node_src, "grp", groups, k)
    else:
        steps = [(k, k + 1) for k in range(0, groups, 2)]
        for k in range(1, groups):
            srcs[k] = move(node_src, "grp", groups, k)

    kinds = 4
    wide = pl.BlockSpec((kinds, pairs, pair, head_dim), lambda r: (r, 0, 0, 0))
    square = pl.BlockSpec((kinds, pairs, pair, pair), lambda r: (r, 0, 0, 0))
    att, msg = pl.pallas_call(
        prepare,
        grid=(relations // kinds,),
        in_specs=[wide, wide],
        out_specs=[square, square],
        out_shape=[jax.ShapeDtypeStruct((relations, pairs, pair, pair), BF)] * 2,
        name="prepare",
        compiler_params=pltpu.CompilerParams(vmem_limit_bytes=LIMIT),
    )(w_att.reshape(relations, pairs, pair, head_dim), w_msg.reshape(relations, pairs, pair, head_dim))

    att, msg = keep(att), keep(msg)
    lists = (
        block_count,
        block_src ^ lax.axis_index("grp"),
        block_dst ^ lax.axis_index("dev"),
        block_type,
        relation_prior,
    )
    state = [
        pltpu.VMEM((owners, width, tile), F32),
        pltpu.VMEM((owners, heads, tile), F32),
        pltpu.VMEM((owners, heads, tile), F32),
    ]
    rows_out = width + 3 * heads
    sent = [pltpu.VMEM((rows_out, tile), BF)] * owners
    for i, slots in enumerate(steps):
        n = len(slots)
        if groups == 8 and i == 2:
            carry = list(carry)
            held = lax.optimization_barrier((srcs[6], srcs[4], carry[2]))
            srcs[6], srcs[4], carry[2] = held
            for k in (7, 5):
                srcs[k] = move(srcs[k - 1], "grp", groups, 1)
        scratch = [
            pltpu.SMEM((2, length + 2), jnp.int32),
            pltpu.VMEM((n * tile, width), BF),
            pltpu.VMEM((n, quads, tile, 2 * pair), BF),
            pltpu.VMEM((n, quads, 2 * pair, tile), BF),
        ]
        cost = pl.CostEstimate(flops=9 * 10**9, bytes_accessed=1 << 20, transcendentals=0)
        tiles = [keep(srcs[k]) for k in slots]
        if i == 0:
            queries, *carry = pl.pallas_call(
                functools.partial(first_phase, shape, slots),
                in_specs=[smem] * 5 + [vmem] * (n + 5 + owners),
                out_specs=[vmem] * 4,
                out_shape=[pltpu.VMEM((owners, width, tile), BF)] + state,
                scratch_shapes=scratch,
                cost_estimate=cost,
            compiler_params=pltpu.CompilerParams(vmem_limit_bytes=LIMIT),
                name="phase0",
            )(*lists, *tiles, w_key, w_value, att, msg, w_query, *[keep(hubs[k]) for k in range(owners)])
            continue
        last = i == len(steps) - 1
        base = 10 + n
        aliases = {} if last else {base + k: k for k in range(3)}
        carry = pl.pallas_call(
            functools.partial(later_phase, shape, slots, last),
            in_specs=[smem] * 5 + [vmem] * (n + 8),
            out_specs=[vmem] * (owners if last else 3),
            out_shape=sent if last else state,
            scratch_shapes=scratch,
            input_output_aliases=aliases,
            cost_estimate=cost,
            compiler_params=pltpu.CompilerParams(vmem_limit_bytes=LIMIT),
            name="phase%d" % i,
        )(*lists, *tiles, w_key, w_value, att, msg, queries, *carry)
    parts = [carry[0]] + [move(carry[k], "dev", owners, k) for k in range(1, owners)]
    return pl.pallas_call(
        functools.partial(combine, owners, heads, head_dim),
        out_shape=jax.ShapeDtypeStruct((tile, width), BF),
        scratch_shapes=[pltpu.VMEM((tile, width), BF)],
        compiler_params=pltpu.CompilerParams(vmem_limit_bytes=LIMIT),
        name="combine",
    )(*[keep(p) for p in parts], w_out)


def solution(mesh):
    rows = P(("grp", "dev"), None)
    placed = (rows, rows) + (P(),) * 7 + (rows,) * 3 + (P(("grp", "dev")),)
    return jax.shard_map(body, mesh=mesh, in_specs=placed, out_specs=rows, check_vma=False)
```

time: 901 us -> 87.4 us (0.10)
  waiting for transfers between devices: 367 us -> 31.4 us
  loops' own time: 145 us -> 0 us
  other arithmetic: 98.3 us -> 0.01 us
  matrix products: 97.9 us -> 0 us
  local copies, waits for them, and re-layouts: 89.5 us -> 4.41 us
  blocking collectives: 81 us -> 0 us
  Pallas kernels: 0 us -> 34.6 us
  starting transfers between devices: 0.13 us -> 15.3 us
  between operations: 13.2 us -> 0.88 us
    unnamed x6 -> x0, waiting for transfers between devices: 274 us -> none
    another operation x1 -> x0, loops' own time: 145 us -> none  [body(): highest, denom, total = lax.fori_loop(0, block_count[0], one_block, init)]
    dot_general x49 -> x0, matrix products: 97.9 us -> none  [the longest x23 50.2 us: one_block(): jnp.einsum('hts,she->the', weight.astype(jnp.bfloat16), message, preferre...]
    all_gather x2 -> x0, waiting for transfers between devices: 92.2 us -> none  [the longest x1 77.1 us: body(): keyval = lax.all_gather(own_kv, 'grp', axis=0, tiled=True)]
    pmax x1 -> x0, blocking collectives: 81 us -> none  [body(): lax.pmax(highest.astype(jnp.bfloat16), 'dev').astype(highest.dtype)]
    dynamic_update_slice x46 -> x0, other arithmetic: 49.1 us -> none  [the longest x23 48.9 us: one_block(): lax.dynamic_update_slice_in_dim(total, old_t * jnp.repeat(factor, head_di...]
    dynamic_slice x46 -> x0, local copies, waits for them, and re-layouts: 41.6 us -> none  [one_block(): lax.dynamic_slice_in_dim(all_queries, start, tile_rows, 0)]
    slice x23 -> x0, local copies, waits for them, and re-layouts: 40.7 us -> none  [one_block(): values = src_rows[:, width:].reshape(tile_rows, heads, head_dim)]
  transfers between devices with their start and end apart: 4 -> 13, of which waited for: 4 -> 5; matrix products, arithmetic and copies ran while one was open for 1% -> 0% of each run, Pallas kernels for 0% -> 30%
where the time goes in v2:
time: 87.4 us; the launch traced here: 86.5 us
  Pallas kernels  34.6 us (40%)
  waiting for transfers between devices  31.4 us (36%)
  starting transfers between devices  15.3 us (18%)
  local copies, waits for them, and re-layouts  4.41 us (5%)
  between operations  0.88 us (1%)
    ppermute x13, waiting for transfers between devices, move(): return lax.ppermute(x, axis, [(i, i ^ k) for i in range(size)])  31.4 us
    pallas_call x3, Pallas kernels, body(): pl.pallas_call(functools.partial(later_phase, shape, slots, last), in_spe...  20.7 us
    ppermute x13, starting transfers between devices, move(): return lax.ppermute(x, axis, [(i, i ^ k) for i in range(size)])  15.3 us
    pallas_call x1, Pallas kernels, body(): pl.pallas_call(prepare, grid=(relations // kinds,), in_specs=[wide, wide]...  6.32 us
    pallas_call x1, Pallas kernels, body(): pl.pallas_call(functools.partial(first_phase, shape, slots), in_specs=[sm...  5.94 us
    unnamed x24, local copies, waits for them, and re-layouts  4.41 us
  transfers between devices with their start and end apart: 13, of which 5 were waited for; matrix products, arithmetic and copies ran while one was open for 0% of the time, Pallas kernels for 30%

profile of v2, /device:TPU:0, one launch (start us, length us, event | category | flops | bytes accessed | tf_op | source)
XLA Modules:
  0.0 86.5 jit_solution(14935605571161024227)
XLA Ops:
  0.0 3.0 %collective-permute-start.6 = (bf16[128,1024]{1,0:T(8,128)(2,1)}, bf16[128,1024]{1,0:T(8,128)(2,1)S(1)}, u32[]{:S(2)}, u32[]{:S(2)}) collective-permute-start(bf16[128,1024]{1,0:T(8,128)(2,1)} %refs_12_.1), channel_id=1, source_target_pairs={{0,2},{1,3},{2,0},{3,1},{4,6},{5,7},{6,4},{7,5},{8,10},{9,11},{10,... | collective-permute-start | bytes 786440 | tf_op jit(solution)/shard_map/ppermute | solution.py:268
  3.0 1.5 %collective-permute-start.4 = (bf16[128,1024]{1,0:T(8,128)(2,1)}, bf16[128,1024]{1,0:T(8,128)(2,1)S(1)}, u32[]{:S(2)}, u32[]{:S(2)}) collective-permute-start(bf16[128,1024]{1,0:T(8,128)(2,1)} %refs_5_.1), channel_id=1, source_target_pairs={{0,4},{4,0},{8,12},{12,8},{16,20},{20,16},{24,28},{28,24},{1,5},{5... | collective-permute-start | bytes 786440 | tf_op jit(solution)/shard_map/ppermute | solution.py:268
  4.5 0.0 collective-permute-start.5
  4.5 5.0 %collective-permute-done.6.refs_14_ = bf16[128,1024]{1,0:T(8,128)(2,1)S(1)} collective-permute-done((bf16[128,1024]{1,0:T(8,128)(2,1)}, bf16[128,1024]{1,0:T(8,128)(2,1)S(1)}, u32[]{:S(2)}, u32[]{:S(2)}) %collective-permute-start.6) | collective-permute-done | bytes 262176 | tf_op jit(solution)/shard_map/ppermute | solution.py:268
  9.5 0.0 collective-permute-start.7
  9.5 1.8 %collective-permute-start.2 = (bf16[128,1024]{1,0:T(8,128)(2,1)}, bf16[128,1024]{1,0:T(8,128)(2,1)S(1)}, u32[]{:S(2)}, u32[]{:S(2)}) collective-permute-start(bf16[128,1024]{1,0:T(8,128)(2,1)} %refs_5_.1), channel_id=1, source_target_pairs={{0,8},{4,12},{8,0},{12,4},{16,24},{20,28},{24,16},{28,20},{1,9},{5... | collective-permute-start | bytes 786440 | tf_op jit(solution)/shard_map/ppermute | solution.py:268
  11.3 1.4 %collective-permute-start.3 = (bf16[128,1024]{1,0:T(8,128)(2,1)}, bf16[128,1024]{1,0:T(8,128)(2,1)S(1)}, u32[]{:S(2)}, u32[]{:S(2)}) collective-permute-start(bf16[128,1024]{1,0:T(8,128)(2,1)} %refs_5_.1), channel_id=1, source_target_pairs={{0,12},{4,8},{8,4},{12,0},{16,28},{20,24},{24,20},{28,16},{1,13},{... | collective-permute-start | bytes 786440 | tf_op jit(solution)/shard_map/ppermute | solution.py:268
  13.3 0.0 copy-start
  13.3 2.2 %copy-done = bf16[16,16,64,64]{3,2,1,0:T(8,128)(2,1)S(1)} copy-done((bf16[16,16,64,64]{3,2,1,0:T(8,128)(2,1)S(1)}, bf16[16,16,64,64]{3,2,1,0:T(8,128)(2,1)}, u32[]{:S(2)}) %copy-start) | copy-done | bytes 2097176
  15.5 2.2 %copy-done.1 = bf16[16,16,64,64]{3,2,1,0:T(8,128)(2,1)S(1)} copy-done((bf16[16,16,64,64]{3,2,1,0:T(8,128)(2,1)S(1)}, bf16[16,16,64,64]{3,2,1,0:T(8,128)(2,1)}, u32[]{:S(2)}) %copy-start.1) | copy-done | bytes 2097176
  17.7 0.0 copy-start.4
  17.7 0.0 copy-start.5
  17.7 0.0 copy-start.6
  17.7 0.0 copy-start.8
  17.7 0.0 copy-start.9
  17.8 6.3 %prepare.1 = (bf16[16,8,128,128]{3,2,1,0:T(8,128)(2,1)S(1)}, bf16[16,8,128,128]{3,2,1,0:T(8,128)(2,1)S(1)}) custom-call(bf16[16,8,128,64]{3,2,1,0:T(8,128)(2,1)S(1)} %bitcast.2, bf16[16,8,128,64]{3,2,1,0:T(8,128)(2,1)S(1)} %bitcast.3), custom_call_target="tpu_custom_call" | custom-call | tf_op jit(solution)/shard_map/prepare/pallas_call | solution.py:287
  24.1 0.0 copy-done.10
  24.1 0.0 copy-done.11
  24.1 0.0 collective-permute-done.4.refs_6_
  24.1 0.0 copy-done.7
  24.1 3.7 %collective-permute-start = (bf16[128,1024]{1,0:T(8,128)(2,1)S(1)}, bf16[128,1024]{1,0:T(8,128)(2,1)S(1)}, u32[]{:S(2)}, u32[]{:S(2)}) collective-permute-start(bf16[128,1024]{1,0:T(8,128)(2,1)S(1)} %copy-done.7), channel_id=1, source_target_pairs={{0,24},{4,28},{8,16},{12,20},{16,8},{20,12},{24,0},{28,4},{1,25},{... | collective-permute-start | bytes 786440 | tf_op jit(solution)/shard_map/ppermute | solution.py:268
  27.8 0.0 collective-permute-done.5.refs_13_
  27.8 0.0 collective-permute-start.1
  27.8 0.0 collective-permute-done.7.refs_15_
  27.8 0.0 copy-done.3
  27.8 0.0 copy-done.4
  27.8 0.0 copy-done.5
  27.9 0.0 copy-done.6
  27.9 0.0 copy-done.8
  27.9 5.9 %phase0.1 = (bf16[4,1024,128]{2,1,0:T(8,128)(2,1)S(1)}, f32[4,1024,128]{2,1,0:T(8,128)S(1)}, f32[4,16,128]{2,1,0:T(8,128)S(1)}, f32[4,16,128]{2,1,0:T(8,128)S(1)}) custom-call(s32[1]{0:T(128)S(6)} %copy.26.refs_0_, s32[1,40]{1,0:T(1,128)S(1)} %get-tuple-element.44.refs_1_, s32[1,40]{1,0:T(1,128)S(1)} %get-tuple-element.43.refs_2_, s32[1,40]{1,0:T(1,128)S(1)} %copy-done.9, ...), custom_call_target="tpu_custom_call" | custom-call | flops 8999999488 | bytes 1048576 | tf_op jit(solution)/shard_map/phase0/pallas_call | solution.py:329
  33.8 0.0 collective-permute-done.2.refs_5_
  33.8 0.0 collective-permute-done.3.refs_6_
  33.8 6.2 %phase1.1 = (f32[4,1024,128]{2,1,0:T(8,128)S(1)}, f32[4,16,128]{2,1,0:T(8,128)S(1)}, f32[4,16,128]{2,1,0:T(8,128)S(1)}) custom-call(s32[1]{0:T(128)S(6)} %copy.26.refs_0_, s32[1,40]{1,0:T(1,128)S(1)} %get-tuple-element.44.refs_1_, s32[1,40]{1,0:T(1,128)S(1)} %get-tuple-element.43.refs_2_, ...), custom_call_target="tpu_custom_call", output_to_operand_aliasing={{0}: (12, {}), {1}: (13, {}), {2}: (14, {})} | custom-call | flops 8999999488 | bytes 1048576 | tf_op jit(solution)/shard_map/phase1/pallas_call | solution.py:343
  40.0 0.0 collective-permute-done.refs_5_
  40.0 10.2 %collective-permute-done.1.refs_6_ = bf16[128,1024]{1,0:T(8,128)(2,1)S(1)} collective-permute-done((bf16[128,1024]{1,0:T(8,128)(2,1)S(1)}, bf16[128,1024]{1,0:T(8,128)(2,1)S(1)}, u32[]{:S(2)}, u32[]{:S(2)}) %collective-permute-start.1) | collective-permute-done | bytes 262176 | tf_op jit(solution)/shard_map/ppermute | solution.py:268
  50.2 0.6 collective-permute-start.8
  50.8 1.5 %collective-permute-start.9 = (bf16[128,1024]{1,0:T(8,128)(2,1)S(1)}, bf16[128,1024]{1,0:T(8,128)(2,1)S(1)}, u32[]{:S(2)}, u32[]{:S(2)}) collective-permute-start(bf16[128,1024]{1,0:T(8,128)(2,1)S(1)} %collective-permute-done.1.refs_6_), channel_id=1, source_target_pairs={{0,4},{4,0},{8,12},{12,8},{16,20},{20,16},{24,28},{28,24},{1,5},{5... | collective-permute-start | bytes 786440 | tf_op jit(solution)/shard_map/ppermute | solution.py:268
  52.3 7.3 %phase2.1 = (f32[4,1024,128]{2,1,0:T(8,128)S(1)}, f32[4,16,128]{2,1,0:T(8,128)S(1)}, f32[4,16,128]{2,1,0:T(8,128)S(1)}) custom-call(s32[1]{0:T(128)S(6)} %copy.26.refs_0_, s32[1,40]{1,0:T(1,128)S(1)} %get-tuple-element.44.refs_1_, s32[1,40]{1,0:T(1,128)S(1)} %get-tuple-element.43.refs_2_, ...), custom_call_target="tpu_custom_call", output_to_operand_aliasing={{0}: (12, {}), {1}: (13, {}), {2}: (14, {})} | custom-call | flops 8999999488 | bytes 1048576 | tf_op jit(solution)/shard_map/phase2/pallas_call | solution.py:343
  59.6 0.0 collective-permute-done.8.refs_5_
  59.6 3.6 %collective-permute-done.9.refs_6_ = bf16[128,1024]{1,0:T(8,128)(2,1)S(1)} collective-permute-done((bf16[128,1024]{1,0:T(8,128)(2,1)S(1)}, bf16[128,1024]{1,0:T(8,128)(2,1)S(1)}, u32[]{:S(2)}, u32[]{:S(2)}) %collective-permute-start.9) | collective-permute-done | bytes 262176 | tf_op jit(solution)/shard_map/ppermute | solution.py:268
  63.2 7.2 %phase3.1 = (bf16[1072,128]{1,0:T(8,128)(2,1)S(1)}, bf16[1072,128]{1,0:T(8,128)(2,1)S(1)}, bf16[1072,128]{1,0:T(8,128)(2,1)S(1)}, bf16[1072,128]{1,0:T(8,128)(2,1)S(1)}) custom-call(s32[1]{0:T(128)S(6)} %copy.26.refs_0_, s32[1,40]{1,0:T(1,128)S(1)} %get-tuple-element.44.refs_1_, s32[1,40]{1,0:T(1,128)S(1)} %get-tuple-element.43.refs_2_, ...), custom_call_target="tpu_custom_call" | custom-call | flops 8999999488 | bytes 1048576 | tf_op jit(solution)/shard_map/phase3/pallas_call | solution.py:343
  70.4 0.1 collective-permute-start.10
  70.5 0.4 collective-permute-start.11
  70.9 1.5 %collective-permute-start.12 = (bf16[1072,128]{1,0:T(8,128)(2,1)S(1)}, bf16[1072,128]{1,0:T(8,128)(2,1)S(1)}, u32[]{:S(2)}, u32[]{:S(2)}) collective-permute-start(bf16[1072,128]{1,0:T(8,128)(2,1)S(1)} %get-tuple-element.42), channel_id=1, source_target_pairs={{0,3},{1,2},{2,1},{3,0},{4,7},{5,6},{6,5},{7,4},{8,11},{9,10},{10,... | collective-permute-start | bytes 823304 | tf_op jit(solution)/shard_map/ppermute | solution.py:268
  72.4 0.0 collective-permute-done.10.refs_1_
  72.4 7.6 %collective-permute-done.11.refs_2_ = bf16[1072,128]{1,0:T(8,128)(2,1)S(1)} collective-permute-done((bf16[1072,128]{1,0:T(8,128)(2,1)S(1)}, bf16[1072,128]{1,0:T(8,128)(2,1)S(1)}, u32[]{:S(2)}, u32[]{:S(2)}) %collective-permute-start.11) | collective-permute-done | bytes 274464 | tf_op jit(solution)/shard_map/ppermute | solution.py:268
  80.0 5.0 %collective-permute-done.12.refs_3_ = bf16[1072,128]{1,0:T(8,128)(2,1)S(1)} collective-permute-done((bf16[1072,128]{1,0:T(8,128)(2,1)S(1)}, bf16[1072,128]{1,0:T(8,128)(2,1)S(1)}, u32[]{:S(2)}, u32[]{:S(2)}) %collective-permute-start.12) | collective-permute-done | bytes 274464 | tf_op jit(solution)/shard_map/ppermute | solution.py:268
  84.9 1.6 %combine.1 = bf16[128,1024]{1,0:T(8,128)(2,1)} custom-call(bf16[1072,128]{1,0:T(8,128)(2,1)S(1)} %get-tuple-element.39.refs_0_, bf16[1072,128]{1,0:T(8,128)(2,1)S(1)} %collective-permute-done.10.refs_1_, bf16[1072,128]{1,0:T(8,128)(2,1)S(1)} %collective-permute-done.11.refs_2_, bf16[1072,128]{1,0:T(8,128)(2,1)S(1)} %collective-permute-done.12.refs_3_, ...), custom_call_target="tpu_custom_call" | custom-call | tf_op jit(solution)/shard_map/combine/pallas_call | solution.py:355
  (9 shorter events, 0.0 us)
Async XLA Ops:
  0.0 9.5 %collective-permute-start.6 = (bf16[128,1024]{1,0:T(8,128)(2,1)}, bf16[128,1024]{1,0:T(8,128)(2,1)S(1)}, u32[]{:S(2)}, u32[]{:S(2)}) collective-permute-start(bf16[128,1024]{1,0:T(8,128)(2,1)} %refs_12_.1), channel_id=1, source_target_pairs={{0,2},{1,3},{2,0},{3,1},{4,6},{5,7},{6,4},{7,5},{8,10},{9,11},{10,... | collective-permute-start | bytes 786440 | tf_op jit(solution)/shard_map/ppermute | solution.py:268
  3.0 21.2 %collective-permute-start.4 = (bf16[128,1024]{1,0:T(8,128)(2,1)}, bf16[128,1024]{1,0:T(8,128)(2,1)S(1)}, u32[]{:S(2)}, u32[]{:S(2)}) collective-permute-start(bf16[128,1024]{1,0:T(8,128)(2,1)} %refs_5_.1), channel_id=1, source_target_pairs={{0,4},{4,0},{8,12},{12,8},{16,20},{20,16},{24,28},{28,24},{1,5},{5... | collective-permute-start | bytes 786440 | tf_op jit(solution)/shard_map/ppermute | solution.py:268
  4.5 23.4 %collective-permute-start.5 = (bf16[128,1024]{1,0:T(8,128)(2,1)}, bf16[128,1024]{1,0:T(8,128)(2,1)S(1)}, u32[]{:S(2)}, u32[]{:S(2)}) collective-permute-start(bf16[128,1024]{1,0:T(8,128)(2,1)} %refs_12_.1), channel_id=1, source_target_pairs={{0,1},{1,0},{2,3},{3,2},{4,5},{5,4},{6,7},{7,6},{8,9},{9,8},{10,11... | collective-permute-start | bytes 786440 | tf_op jit(solution)/shard_map/ppermute | solution.py:268
  9.5 18.3 %collective-permute-start.7 = (bf16[128,1024]{1,0:T(8,128)(2,1)S(1)}, bf16[128,1024]{1,0:T(8,128)(2,1)S(1)}, u32[]{:S(2)}, u32[]{:S(2)}) collective-permute-start(bf16[128,1024]{1,0:T(8,128)(2,1)S(1)} %collective-permute-done.6.refs_14_), channel_id=1, source_target_pairs={{0,1},{1,0},{2,3},{3,2},{4,5},{5,4},{6,7},{7,6},{8,9},{9,8},{10,11... | collective-permute-start | bytes 786440 | tf_op jit(solution)/shard_map/ppermute | solution.py:268
  9.5 24.3 %collective-permute-start.2 = (bf16[128,1024]{1,0:T(8,128)(2,1)}, bf16[128,1024]{1,0:T(8,128)(2,1)S(1)}, u32[]{:S(2)}, u32[]{:S(2)}) collective-permute-start(bf16[128,1024]{1,0:T(8,128)(2,1)} %refs_5_.1), channel_id=1, source_target_pairs={{0,8},{4,12},{8,0},{12,4},{16,24},{20,28},{24,16},{28,20},{1,9},{5... | collective-permute-start | bytes 786440 | tf_op jit(solution)/shard_map/ppermute | solution.py:268
  11.3 22.6 %collective-permute-start.3 = (bf16[128,1024]{1,0:T(8,128)(2,1)}, bf16[128,1024]{1,0:T(8,128)(2,1)S(1)}, u32[]{:S(2)}, u32[]{:S(2)}) collective-permute-start(bf16[128,1024]{1,0:T(8,128)(2,1)} %refs_5_.1), channel_id=1, source_target_pairs={{0,12},{4,8},{8,4},{12,0},{16,28},{20,24},{24,20},{28,16},{1,13},{... | collective-permute-start | bytes 786440 | tf_op jit(solution)/shard_map/ppermute | solution.py:268
  13.3 2.2 %copy-start = (bf16[16,16,64,64]{3,2,1,0:T(8,128)(2,1)S(1)}, bf16[16,16,64,64]{3,2,1,0:T(8,128)(2,1)}, u32[]{:S(2)}) copy-start(bf16[16,16,64,64]{3,2,1,0:T(8,128)(2,1)} %param.19) | copy-start | bytes 6291460
  15.5 2.2 %copy-start.1 = (bf16[16,16,64,64]{3,2,1,0:T(8,128)(2,1)S(1)}, bf16[16,16,64,64]{3,2,1,0:T(8,128)(2,1)}, u32[]{:S(2)}) copy-start(bf16[16,16,64,64]{3,2,1,0:T(8,128)(2,1)} %param.20) | copy-start | bytes 6291460
  17.7 6.4 %copy-start.10 = (s32[1,40]{1,0:T(1,128)S(1)}, s32[1,40]{1,0:T(1,128)}, u32[]{:S(2)}) copy-start(s32[1,40]{1,0:T(1,128)} %param.23) | copy-start | bytes 484
  17.7 6.4 %copy-start.11 = (s32[1,40]{1,0:T(1,128)S(1)}, s32[1,40]{1,0:T(1,128)}, u32[]{:S(2)}) copy-start(s32[1,40]{1,0:T(1,128)} %param.22) | copy-start | bytes 484
  17.7 6.4 %copy-start.7 = (bf16[128,1024]{1,0:T(8,128)(2,1)S(1)}, bf16[128,1024]{1,0:T(8,128)(2,1)}, u32[]{:S(2)}) copy-start(bf16[128,1024]{1,0:T(8,128)(2,1)} %refs_5_.1) | copy-start | bytes 786436
  17.7 10.1 %copy-start.3 = (bf16[1024,1024]{1,0:T(8,128)(2,1)S(1)}, bf16[1024,1024]{1,0:T(8,128)(2,1)}, u32[]{:S(2)}) copy-start(bf16[1024,1024]{1,0:T(8,128)(2,1)} %refs_11_.1) | copy-start | bytes 6291460
  17.7 10.1 %copy-start.4 = (bf16[1024,1024]{1,0:T(8,128)(2,1)S(1)}, bf16[1024,1024]{1,0:T(8,128)(2,1)}, u32[]{:S(2)}) copy-start(bf16[1024,1024]{1,0:T(8,128)(2,1)} %refs_7_.7) | copy-start | bytes 6291460
  17.7 10.1 %copy-start.5 = (bf16[1024,1024]{1,0:T(8,128)(2,1)S(1)}, bf16[1024,1024]{1,0:T(8,128)(2,1)}, u32[]{:S(2)}) copy-start(bf16[1024,1024]{1,0:T(8,128)(2,1)} %refs_8_.7) | copy-start | bytes 6291460
  17.7 10.1 %copy-start.6 = (bf16[128,1024]{1,0:T(8,128)(2,1)S(1)}, bf16[128,1024]{1,0:T(8,128)(2,1)}, u32[]{:S(2)}) copy-start(bf16[128,1024]{1,0:T(8,128)(2,1)} %refs_12_.1) | copy-start | bytes 786436
  17.7 10.1 %copy-start.8 = (f32[16,16]{1,0:T(8,128)S(1)}, f32[16,16]{1,0:T(8,128)}, u32[]{:S(2)}) copy-start(f32[16,16]{1,0:T(8,128)} %refs_4_.8) | copy-start | bytes 3076
  17.7 10.1 %copy-start.9 = (s32[1,40]{1,0:T(1,128)S(1)}, s32[1,40]{1,0:T(1,128)}, u32[]{:S(2)}) copy-start(s32[1,40]{1,0:T(1,128)} %refs_3_.7) | copy-start | bytes 484
  24.1 15.9 %collective-permute-start = (bf16[128,1024]{1,0:T(8,128)(2,1)S(1)}, bf16[128,1024]{1,0:T(8,128)(2,1)S(1)}, u32[]{:S(2)}, u32[]{:S(2)}) collective-permute-start(bf16[128,1024]{1,0:T(8,128)(2,1)S(1)} %copy-done.7), channel_id=1, source_target_pairs={{0,24},{4,28},{8,16},{12,20},{16,8},{20,12},{24,0},{28,4},{1,25},{... | collective-permute-start | bytes 786440 | tf_op jit(solution)/shard_map/ppermute | solution.py:268
  27.8 22.4 %collective-permute-start.1 = (bf16[128,1024]{1,0:T(8,128)(2,1)S(1)}, bf16[128,1024]{1,0:T(8,128)(2,1)S(1)}, u32[]{:S(2)}, u32[]{:S(2)}) collective-permute-start(bf16[128,1024]{1,0:T(8,128)(2,1)S(1)} %copy-done.7), channel_id=1, source_target_pairs={{0,16},{4,20},{8,24},{12,28},{16,0},{20,4},{24,8},{28,12},{1,17},{... | collective-permute-start | bytes 786440 | tf_op jit(solution)/shard_map/ppermute | solution.py:268
  50.2 9.4 %collective-permute-start.8 = (bf16[128,1024]{1,0:T(8,128)(2,1)S(1)}, bf16[128,1024]{1,0:T(8,128)(2,1)S(1)}, u32[]{:S(2)}, u32[]{:S(2)}) collective-permute-start(bf16[128,1024]{1,0:T(8,128)(2,1)S(1)} %collective-permute-done.refs_5_), channel_id=1, source_target_pairs={{0,4},{4,0},{8,12},{12,8},{16,20},{20,16},{24,28},{28,24},{1,5},{5... | collective-permute-start | bytes 786440 | tf_op jit(solution)/shard_map/ppermute | solution.py:268
  50.8 12.4 %collective-permute-start.9 = (bf16[128,1024]{1,0:T(8,128)(2,1)S(1)}, bf16[128,1024]{1,0:T(8,128)(2,1)S(1)}, u32[]{:S(2)}, u32[]{:S(2)}) collective-permute-start(bf16[128,1024]{1,0:T(8,128)(2,1)S(1)} %collective-permute-done.1.refs_6_), channel_id=1, source_target_pairs={{0,4},{4,0},{8,12},{12,8},{16,20},{20,16},{24,28},{28,24},{1,5},{5... | collective-permute-start | bytes 786440 | tf_op jit(solution)/shard_map/ppermute | solution.py:268
  63.2 21.7 %copy-start.2 = (bf16[1024,1024]{1,0:T(8,128)(2,1)S(1)}, bf16[1024,1024]{1,0:T(8,128)(2,1)}, u32[]{:S(2)}) copy-start(bf16[1024,1024]{1,0:T(8,128)(2,1)} %refs_4_.9) | copy-start | bytes 6291460
  70.4 1.9 %collective-permute-start.10 = (bf16[1072,128]{1,0:T(8,128)(2,1)S(1)}, bf16[1072,128]{1,0:T(8,128)(2,1)S(1)}, u32[]{:S(2)}, u32[]{:S(2)}) collective-permute-start(bf16[1072,128]{1,0:T(8,128)(2,1)S(1)} %get-tuple-element.40), channel_id=1, source_target_pairs={{0,1},{1,0},{2,3},{3,2},{4,5},{5,4},{6,7},{7,6},{8,9},{9,8},{10,11... | collective-permute-start | bytes 823304 | tf_op jit(solution)/shard_map/ppermute | solution.py:268
  70.5 9.4 %collective-permute-start.11 = (bf16[1072,128]{1,0:T(8,128)(2,1)S(1)}, bf16[1072,128]{1,0:T(8,128)(2,1)S(1)}, u32[]{:S(2)}, u32[]{:S(2)}) collective-permute-start(bf16[1072,128]{1,0:T(8,128)(2,1)S(1)} %get-tuple-element.41), channel_id=1, source_target_pairs={{0,2},{1,3},{2,0},{3,1},{4,6},{5,7},{6,4},{7,5},{8,10},{9,11},{10,... | collective-permute-start | bytes 823304 | tf_op jit(solution)/shard_map/ppermute | solution.py:268
  70.9 14.0 %collective-permute-start.12 = (bf16[1072,128]{1,0:T(8,128)(2,1)S(1)}, bf16[1072,128]{1,0:T(8,128)(2,1)S(1)}, u32[]{:S(2)}, u32[]{:S(2)}) collective-permute-start(bf16[1072,128]{1,0:T(8,128)(2,1)S(1)} %get-tuple-element.42), channel_id=1, source_target_pairs={{0,3},{1,2},{2,1},{3,0},{4,7},{5,6},{6,5},{7,4},{8,11},{9,10},{10,... | collective-permute-start | bytes 823304 | tf_op jit(solution)/shard_map/ppermute | solution.py:268

commit v3 on v2

--- a/solution.py
+++ b/solution.py
@@ -14,6 +14,7 @@
 BLOCKS = 2
 LAGS = (4, 8, 12)
 LIMIT = 16 << 20
+COST = 10**6
 
 
 def split3(x):
@@ -29,16 +30,21 @@
     row = lax.broadcasted_iota(jnp.int32, (pair, head_dim), 0)
     col = lax.broadcasted_iota(jnp.int32, (pair, head_dim), 1)
     twice = jnp.where((row & (head_dim - 1)) == col, 1.0, 0.0).astype(BF)
-    r2 = lax.broadcasted_iota(jnp.int32, (pair, pair), 0)
-    c2 = lax.broadcasted_iota(jnp.int32, (pair, pair), 1)
-    same = (r2 < head_dim) == (c2 < head_dim)
-    dims = (((1,), (1,)), ((), ()))
+    r2 = lax.broadcasted_iota(jnp.int32, (pair, 2 * pair), 0)
+    c2 = lax.broadcasted_iota(jnp.int32, (pair, 2 * pair), 1)
+    same = (r2 < head_dim) == ((c2 & (pair - 1)) < head_dim)
+    none = jnp.zeros((head_dim, head_dim), BF)
     for r in range(kinds):
         for h in range(pairs):
-            a = lax.dot_general(att[r, h], twice, dims, preferred_element_type=F32)
-            att_out[r, h] = jnp.where(same, a, 0.0).astype(BF)
-            m = lax.dot_general(twice, msg[r, h], dims, preferred_element_type=F32)
-            msg_out[r, h] = jnp.where(same, m, 0.0).astype(BF)
+            upper = jnp.concatenate([att[r, h, :head_dim, :], none], axis=1)
+            lower = jnp.concatenate([none, att[r, h, head_dim:, :]], axis=1)
+            att_out[r, h] = jnp.concatenate([upper, lower], axis=0)
+        for h in range(0, pairs, 2):
+            both = msg[r, h : h + 2].reshape(2 * pair, head_dim)
+            m = lax.dot_general(twice, both, (((1,), (1,)), ((), ())), preferred_element_type=F32)
+            m = jnp.where(same, m, 0.0).astype(BF)
+            msg_out[r, h] = m[:, :pair]
+            msg_out[r, h + 1] = m[:, pair:]
 
 
 def run_blocks(
@@ -260,6 +266,7 @@
     length = block_src.shape[1]
     shape = (owners, heads, tile, head_dim)
     smem = pl.BlockSpec(memory_space=pltpu.SMEM)
+    apart = lambda x: pltpu.with_memory_space_constraint(x, pltpu.HBM)
     keep = lambda x: pltpu.with_memory_space_constraint(x, pltpu.VMEM)
     w_query, w_key, w_value, w_out = (keep(w) for w in (w_query, w_key, w_value, w_out))
     vmem = pl.BlockSpec(memory_space=pltpu.VMEM)
@@ -268,13 +275,12 @@
         return lax.ppermute(x, axis, [(i, i ^ k) for i in range(size)])
 
     hubs = {0: hub_feat}
-    for k in range(1, owners):
-        far = k > 1 and k % 2 == 1
-        hubs[k] = move(hubs[k - 1] if far else hub_feat, "dev", owners, 1 if far else k)
+    for k in range(2, owners, 2):
+        hubs[k] = move(hub_feat, "dev", owners, k)
     srcs = {0: node_src}
     if groups == 8:
         steps = [(0, 1), (2, 3), (6, 4), (7, 5)]
-        for k in (1, 2, 3, 6, 4):
+        for k in (1, 6, 2, 3):
             srcs[k] = move(node_src, "grp", groups, k)
     else:
         steps = [(k, k + 1) for k in range(0, groups, 2)]
@@ -292,8 +298,15 @@
         out_shape=[jax.ShapeDtypeStruct((relations, pairs, pair, pair), BF)] * 2,
         name="prepare",
         compiler_params=pltpu.CompilerParams(vmem_limit_bytes=LIMIT),
-    )(w_att.reshape(relations, pairs, pair, head_dim), w_msg.reshape(relations, pairs, pair, head_dim))
-
+    )(*[apart(w.reshape(relations, pairs, pair, head_dim)) for w in (w_att, w_msg)])
+    held = lax.optimization_barrier((att, srcs[1], *[hubs[k] for k in range(0, owners, 2)]))
+    att, srcs[1], near = held[0], held[1], held[2:]
+    for k in range(0, owners, 2):
+        hubs[k] = near[k // 2]
+        hubs[k + 1] = move(hubs[k], "dev", owners, 1)
+    if groups == 8:
+        source, hubs[1] = lax.optimization_barrier((node_src, hubs[1]))
+        srcs[4] = move(source, "grp", groups, 4)
     att, msg = keep(att), keep(msg)
     lists = (
         block_count,
@@ -323,7 +336,7 @@
             pltpu.VMEM((n, quads, tile, 2 * pair), BF),
             pltpu.VMEM((n, quads, 2 * pair, tile), BF),
         ]
-        cost = pl.CostEstimate(flops=9 * 10**9, bytes_accessed=1 << 20, transcendentals=0)
+        cost = pl.CostEstimate(flops=COST, bytes_accessed=1024, transcendentals=0)
         tiles = [keep(srcs[k]) for k in slots]
         if i == 0:
             queries, *carry = pl.pallas_call(

time: 87.4 us -> 84.7 us (0.969)
  the two profiles are of different devices: /device:TPU:0 before, /device:TPU:17 now
where the time goes in v3:
time: 84.7 us; the launch traced here: 84.5 us
  Pallas kernels  36.3 us (43%)
  starting transfers between devices  20.8 us (25%)
  waiting for transfers between devices  13.3 us (16%)
  local copies, waits for them, and re-layouts  13.2 us (16%)
  between operations  0.86 us (1%)
    pallas_call x3, Pallas kernels, body(): pl.pallas_call(functools.partial(later_phase, shape, slots, last), in_spe...  23.4 us
    ppermute x13, starting transfers between devices, move(): return lax.ppermute(x, axis, [(i, i ^ k) for i in range(size)])  20.8 us
    ppermute x13, waiting for transfers between devices, move(): return lax.ppermute(x, axis, [(i, i ^ k) for i in range(size)])  13.3 us
    unnamed x32, local copies, waits for them, and re-layouts  13.2 us
    pallas_call x1, Pallas kernels, body(): pl.pallas_call(functools.partial(first_phase, shape, slots), in_specs=[sm...  6.29 us
    pallas_call x1, Pallas kernels, body(): pl.pallas_call(prepare, grid=(relations // kinds,), in_specs=[wide, wide]...  5.04 us
  transfers between devices with their start and end apart: 13, of which 3 were waited for; matrix products, arithmetic and copies ran while one was open for 0% of the time, Pallas kernels for 31%

profile of v3, /device:TPU:17, one launch (start us, length us, event | category | flops | bytes accessed | tf_op | source)
XLA Modules:
  0.0 84.5 jit_solution(4538232151666861338)
XLA Ops:
  0.0 1.2 %collective-permute-start.1 = (bf16[128,1024]{1,0:T(8,128)(2,1)}, bf16[128,1024]{1,0:T(8,128)(2,1)S(1)}, u32[]{:S(2)}, u32[]{:S(2)}) collective-permute-start(bf16[128,1024]{1,0:T(8,128)(2,1)} %refs_5_.1), channel_id=1, source_target_pairs={{0,4},{4,0},{8,12},{12,8},{16,20},{20,16},{24,28},{28,24},{1,5},{5... | collective-permute-start | bytes 786440 | tf_op jit(solution)/shard_map/ppermute | solution.py:275
  1.2 1.2 %collective-permute-start.2 = (bf16[128,1024]{1,0:T(8,128)(2,1)}, bf16[128,1024]{1,0:T(8,128)(2,1)}, u32[]{:S(2)}, u32[]{:S(2)}) collective-permute-start(bf16[128,1024]{1,0:T(8,128)(2,1)} %refs_12_), channel_id=1, source_target_pairs={{0,2},{1,3},{2,0},{3,1},{4,6},{5,7},{6,4},{7,5},{8,10},{9,11},{10,... | collective-permute-start | bytes 786440 | tf_op jit(solution)/shard_map/ppermute | solution.py:275
  2.5 0.0 copy-start.4
  2.5 0.0 copy-start.12
  2.5 5.0 %prepare.1 = (bf16[16,8,128,128]{3,2,1,0:T(8,128)(2,1)S(1)}, bf16[16,8,128,128]{3,2,1,0:T(8,128)(2,1)S(1)}) custom-call(bf16[16,8,128,64]{3,2,1,0:T(8,128)(2,1)} %bitcast.2, bf16[16,8,128,64]{3,2,1,0:T(8,128)(2,1)} %bitcast.3), custom_call_target="tpu_custom_call" | custom-call | tf_op jit(solution)/shard_map/prepare/pallas_call | solution.py:293
  7.6 1.9 %copy-done = bf16[16,8,128,128]{3,2,1,0:T(8,128)(2,1)} copy-done((bf16[16,8,128,128]{3,2,1,0:T(8,128)(2,1)}, bf16[16,8,128,128]{3,2,1,0:T(8,128)(2,1)S(1)}, u32[]{:S(2)}) %copy-start) | copy-done | bytes 4194328
  9.5 2.0 %copy-done.2 = bf16[16,8,128,128]{3,2,1,0:T(8,128)(2,1)} copy-done((bf16[16,8,128,128]{3,2,1,0:T(8,128)(2,1)}, bf16[16,8,128,128]{3,2,1,0:T(8,128)(2,1)S(1)}, u32[]{:S(2)}) %copy-start.2) | copy-done | bytes 4194328
  11.5 0.0 collective-permute-done.1.refs_6_
  11.5 0.0 collective-permute-done.2.refs_14_
  11.5 1.3 %collective-permute-start.3 = (bf16[128,1024]{1,0:T(8,128)(2,1)S(1)}, bf16[128,1024]{1,0:T(8,128)(2,1)S(1)}, u32[]{:S(2)}, u32[]{:S(2)}) collective-permute-start(bf16[128,1024]{1,0:T(8,128)(2,1)S(1)} %copy-done.8), channel_id=1, source_target_pairs={{0,1},{1,0},{2,3},{3,2},{4,5},{5,4},{6,7},{7,6},{8,9},{9,8},{10,11... | collective-permute-start | bytes 786440 | tf_op jit(solution)/shard_map/ppermute | solution.py:275
  12.8 0.1 collective-permute-start.7
  12.9 0.0 copy-done.9
  12.9 1.3 %collective-permute-start.5 = (bf16[128,1024]{1,0:T(8,128)(2,1)S(1)}, bf16[128,1024]{1,0:T(8,128)(2,1)}, u32[]{:S(2)}, u32[]{:S(2)}) collective-permute-start(bf16[128,1024]{1,0:T(8,128)(2,1)S(1)} %copy-done.9), channel_id=1, source_target_pairs={{0,8},{4,12},{8,0},{12,4},{16,24},{20,28},{24,16},{28,20},{1,9},{5... | collective-permute-start | bytes 786440 | tf_op jit(solution)/shard_map/ppermute | solution.py:275
  14.2 0.1 collective-permute-start.6
  14.4 0.2 collective-permute-start
  14.5 0.0 collective-permute-done.3.refs_13_
  14.5 0.7 copy-done.10
  15.2 3.2 %collective-permute-start.4 = (bf16[128,1024]{1,0:T(8,128)(2,1)S(1)}, bf16[128,1024]{1,0:T(8,128)(2,1)S(1)}, u32[]{:S(2)}, u32[]{:S(2)}) collective-permute-start(bf16[128,1024]{1,0:T(8,128)(2,1)S(1)} %copy-done.9), channel_id=1, source_target_pairs={{0,16},{4,20},{8,24},{12,28},{16,0},{20,4},{24,8},{28,12},{1,17},{... | collective-permute-start | bytes 786440 | tf_op jit(solution)/shard_map/ppermute | solution.py:275
  19.1 0.0 collective-permute-done.7.refs_15_
  19.1 0.0 copy-done.4
  19.2 0.0 copy-done.12
  19.2 0.0 copy-done.13
  19.2 0.0 copy-start.1
  19.2 2.2 %copy-done.1 = bf16[16,8,128,128]{3,2,1,0:T(8,128)(2,1)S(1)} copy-done((bf16[16,8,128,128]{3,2,1,0:T(8,128)(2,1)S(1)}, bf16[16,8,128,128]{3,2,1,0:T(8,128)(2,1)}, u32[]{:S(2)}) %copy-start.1) | copy-done | bytes 4194328
  21.4 2.2 %copy-done.3 = bf16[16,8,128,128]{3,2,1,0:T(8,128)(2,1)S(1)} copy-done((bf16[16,8,128,128]{3,2,1,0:T(8,128)(2,1)S(1)}, bf16[16,8,128,128]{3,2,1,0:T(8,128)(2,1)}, u32[]{:S(2)}) %copy-start.3) | copy-done | bytes 4194328
  23.6 1.6 %copy-done.5 = bf16[1024,1024]{1,0:T(8,128)(2,1)S(1)} copy-done((bf16[1024,1024]{1,0:T(8,128)(2,1)S(1)}, bf16[1024,1024]{1,0:T(8,128)(2,1)}, u32[]{:S(2)}) %copy-start.5) | copy-done | bytes 2097176
  25.1 1.6 %copy-done.7 = bf16[1024,1024]{1,0:T(8,128)(2,1)S(1)} copy-done((bf16[1024,1024]{1,0:T(8,128)(2,1)S(1)}, bf16[1024,1024]{1,0:T(8,128)(2,1)}, u32[]{:S(2)}) %copy-start.7) | copy-done | bytes 2097176
  26.7 0.9 %copy-done.11 = bf16[128,1024]{1,0:T(8,128)(2,1)S(1)} copy-done((bf16[128,1024]{1,0:T(8,128)(2,1)S(1)}, bf16[128,1024]{1,0:T(8,128)(2,1)}, u32[]{:S(2)}) %copy-start.11) | copy-done | bytes 262168
  27.7 6.3 %phase0.1 = (bf16[4,1024,128]{2,1,0:T(8,128)(2,1)S(1)}, f32[4,1024,128]{2,1,0:T(8,128)S(1)}, f32[4,16,128]{2,1,0:T(8,128)S(1)}, f32[4,16,128]{2,1,0:T(8,128)S(1)}) custom-call(s32[1]{0:T(128)S(6)} %copy.26.refs_0_, s32[1,40]{1,0:T(1,128)S(1)} %get-tuple-element.56.refs_1_, s32[1,40]{1,0:T(1,128)S(1)} %get-tuple-element.55.refs_2_, s32[1,40]{1,0:T(1,128)S(1)} %copy-done.13, ...), custom_call_target="tpu_custom_call" | custom-call | flops 1000000 | bytes 1024 | tf_op jit(solution)/shard_map/phase0/pallas_call | solution.py:342
  34.0 0.0 collective-permute-done.5.refs_5_
  34.0 0.8 collective-permute-done.6.refs_6_
  34.8 7.7 %phase1.1 = (f32[4,1024,128]{2,1,0:T(8,128)S(1)}, f32[4,16,128]{2,1,0:T(8,128)S(1)}, f32[4,16,128]{2,1,0:T(8,128)S(1)}) custom-call(s32[1]{0:T(128)S(6)} %copy.26.refs_0_, s32[1,40]{1,0:T(1,128)S(1)} %get-tuple-element.56.refs_1_, s32[1,40]{1,0:T(1,128)S(1)} %get-tuple-element.55.refs_2_, ...), custom_call_target="tpu_custom_call", output_to_operand_aliasing={{0}: (12, {}), {1}: (13, {}), {2}: (14, {})} | custom-call | flops 1000000 | bytes 1024 | tf_op jit(solution)/shard_map/phase1/pallas_call | solution.py:356
  42.5 0.0 collective-permute-done.refs_5_
  42.5 0.0 collective-permute-done.4.refs_6_
  42.5 0.1 collective-permute-start.8
  42.6 1.5 %collective-permute-start.9 = (bf16[128,1024]{1,0:T(8,128)(2,1)S(1)}, bf16[128,1024]{1,0:T(8,128)(2,1)S(1)}, u32[]{:S(2)}, u32[]{:S(2)}) collective-permute-start(bf16[128,1024]{1,0:T(8,128)(2,1)S(1)} %collective-permute-done.4.refs_6_), channel_id=1, source_target_pairs={{0,4},{4,0},{8,12},{12,8},{16,20},{20,16},{24,28},{28,24},{1,5},{5... | collective-permute-start | bytes 786440 | tf_op jit(solution)/shard_map/ppermute | solution.py:275
  44.1 7.3 %phase2.1 = (f32[4,1024,128]{2,1,0:T(8,128)S(1)}, f32[4,16,128]{2,1,0:T(8,128)S(1)}, f32[4,16,128]{2,1,0:T(8,128)S(1)}) custom-call(s32[1]{0:T(128)S(6)} %copy.26.refs_0_, s32[1,40]{1,0:T(1,128)S(1)} %get-tuple-element.56.refs_1_, s32[1,40]{1,0:T(1,128)S(1)} %get-tuple-element.55.refs_2_, ...), custom_call_target="tpu_custom_call", output_to_operand_aliasing={{0}: (12, {}), {1}: (13, {}), {2}: (14, {})} | custom-call | flops 1000000 | bytes 1024 | tf_op jit(solution)/shard_map/phase2/pallas_call | solution.py:356
  51.4 0.0 collective-permute-done.8.refs_5_
  51.4 0.0 collective-permute-done.9.refs_6_
  51.4 0.0 copy-start.6
  51.4 8.4 %phase3.1 = (bf16[1072,128]{1,0:T(8,128)(2,1)S(1)}, bf16[1072,128]{1,0:T(8,128)(2,1)S(1)}, bf16[1072,128]{1,0:T(8,128)(2,1)S(1)}, bf16[1072,128]{1,0:T(8,128)(2,1)S(1)}) custom-call(s32[1]{0:T(128)S(6)} %copy.26.refs_0_, s32[1,40]{1,0:T(1,128)S(1)} %get-tuple-element.56.refs_1_, s32[1,40]{1,0:T(1,128)S(1)} %get-tuple-element.55.refs_2_, ...), custom_call_target="tpu_custom_call" | custom-call | flops 1000000 | bytes 1024 | tf_op jit(solution)/shard_map/phase3/pallas_call | solution.py:356
  59.8 8.9 %collective-permute-start.10 = (bf16[1072,128]{1,0:T(8,128)(2,1)S(1)}, bf16[1072,128]{1,0:T(8,128)(2,1)S(1)}, u32[]{:S(2)}, u32[]{:S(2)}) collective-permute-start(bf16[1072,128]{1,0:T(8,128)(2,1)S(1)} %get-tuple-element.52), channel_id=1, source_target_pairs={{0,1},{1,0},{2,3},{3,2},{4,5},{5,4},{6,7},{7,6},{8,9},{9,8},{10,11... | collective-permute-start | bytes 823304 | tf_op jit(solution)/shard_map/ppermute | solution.py:275
  68.7 0.0 collective-permute-start.11
  68.7 1.7 %collective-permute-start.12 = (bf16[1072,128]{1,0:T(8,128)(2,1)S(1)}, bf16[1072,128]{1,0:T(8,128)(2,1)S(1)}, u32[]{:S(2)}, u32[]{:S(2)}) collective-permute-start(bf16[1072,128]{1,0:T(8,128)(2,1)S(1)} %get-tuple-element.54), channel_id=1, source_target_pairs={{0,3},{1,2},{2,1},{3,0},{4,7},{5,6},{6,5},{7,4},{8,11},{9,10},{10,... | collective-permute-start | bytes 823304 | tf_op jit(solution)/shard_map/ppermute | solution.py:275
  70.4 0.0 collective-permute-done.10.refs_1_
  70.4 6.4 %collective-permute-done.11.refs_2_ = bf16[1072,128]{1,0:T(8,128)(2,1)S(1)} collective-permute-done((bf16[1072,128]{1,0:T(8,128)(2,1)S(1)}, bf16[1072,128]{1,0:T(8,128)(2,1)S(1)}, u32[]{:S(2)}, u32[]{:S(2)}) %collective-permute-start.11) | collective-permute-done | bytes 274464 | tf_op jit(solution)/shard_map/ppermute | solution.py:275
  76.8 6.0 %collective-permute-done.12.refs_3_ = bf16[1072,128]{1,0:T(8,128)(2,1)S(1)} collective-permute-done((bf16[1072,128]{1,0:T(8,128)(2,1)S(1)}, bf16[1072,128]{1,0:T(8,128)(2,1)S(1)}, u32[]{:S(2)}, u32[]{:S(2)}) %collective-permute-start.12) | collective-permute-done | bytes 274464 | tf_op jit(solution)/shard_map/ppermute | solution.py:275
  82.9 1.6 %combine.1 = bf16[128,1024]{1,0:T(8,128)(2,1)} custom-call(bf16[1072,128]{1,0:T(8,128)(2,1)S(1)} %get-tuple-element.51.refs_0_, bf16[1072,128]{1,0:T(8,128)(2,1)S(1)} %collective-permute-done.10.refs_1_, bf16[1072,128]{1,0:T(8,128)(2,1)S(1)} %collective-permute-done.11.refs_2_, bf16[1072,128]{1,0:T(8,128)(2,1)S(1)} %collective-permute-done.12.refs_3_, ...), custom_call_target="tpu_custom_call" | custom-call | tf_op jit(solution)/shard_map/combine/pallas_call | solution.py:368
  (17 shorter events, 0.0 us)
Async XLA Ops:
  0.0 11.5 %collective-permute-start.1 = (bf16[128,1024]{1,0:T(8,128)(2,1)}, bf16[128,1024]{1,0:T(8,128)(2,1)S(1)}, u32[]{:S(2)}, u32[]{:S(2)}) collective-permute-start(bf16[128,1024]{1,0:T(8,128)(2,1)} %refs_5_.1), channel_id=1, source_target_pairs={{0,4},{4,0},{8,12},{12,8},{16,20},{20,16},{24,28},{28,24},{1,5},{5... | collective-permute-start | bytes 786440 | tf_op jit(solution)/shard_map/ppermute | solution.py:275
  1.2 10.3 %collective-permute-start.2 = (bf16[128,1024]{1,0:T(8,128)(2,1)}, bf16[128,1024]{1,0:T(8,128)(2,1)}, u32[]{:S(2)}, u32[]{:S(2)}) collective-permute-start(bf16[128,1024]{1,0:T(8,128)(2,1)} %refs_12_), channel_id=1, source_target_pairs={{0,2},{1,3},{2,0},{3,1},{4,6},{5,7},{6,4},{7,5},{8,10},{9,11},{10,... | collective-permute-start | bytes 786440 | tf_op jit(solution)/shard_map/ppermute | solution.py:275
  2.5 9.1 %copy-start.8 = (bf16[128,1024]{1,0:T(8,128)(2,1)S(1)}, bf16[128,1024]{1,0:T(8,128)(2,1)}, u32[]{:S(2)}) copy-start(bf16[128,1024]{1,0:T(8,128)(2,1)} %refs_12_) | copy-start | bytes 786436
  2.5 10.5 %copy-start.9 = (bf16[128,1024]{1,0:T(8,128)(2,1)S(1)}, bf16[128,1024]{1,0:T(8,128)(2,1)}, u32[]{:S(2)}) copy-start(bf16[128,1024]{1,0:T(8,128)(2,1)} %refs_5_.1) | copy-start | bytes 786436
  2.5 16.6 %copy-start.14 = (s32[1,40]{1,0:T(1,128)S(1)}, s32[1,40]{1,0:T(1,128)}, u32[]{:S(2)}) copy-start(s32[1,40]{1,0:T(1,128)} %param.23) | copy-start | bytes 484
  2.5 16.7 %copy-start.15 = (s32[1,40]{1,0:T(1,128)S(1)}, s32[1,40]{1,0:T(1,128)}, u32[]{:S(2)}) copy-start(s32[1,40]{1,0:T(1,128)} %param.22) | copy-start | bytes 484
  2.5 16.7 %copy-start.4 = (bf16[1024,1024]{1,0:T(8,128)(2,1)S(1)}, bf16[1024,1024]{1,0:T(8,128)(2,1)}, u32[]{:S(2)}) copy-start(bf16[1024,1024]{1,0:T(8,128)(2,1)} %refs_7_.7) | copy-start | bytes 6291460
  2.5 16.7 %copy-start.12 = (f32[16,16]{1,0:T(8,128)S(1)}, f32[16,16]{1,0:T(8,128)}, u32[]{:S(2)}) copy-start(f32[16,16]{1,0:T(8,128)} %refs_4_.8) | copy-start | bytes 3076
  2.5 16.7 %copy-start.13 = (s32[1,40]{1,0:T(1,128)S(1)}, s32[1,40]{1,0:T(1,128)}, u32[]{:S(2)}) copy-start(s32[1,40]{1,0:T(1,128)} %refs_3_.7) | copy-start | bytes 484
  7.5 2.0 %copy-start = (bf16[16,8,128,128]{3,2,1,0:T(8,128)(2,1)}, bf16[16,8,128,128]{3,2,1,0:T(8,128)(2,1)S(1)}, u32[]{:S(2)}) copy-start(bf16[16,8,128,128]{3,2,1,0:T(8,128)(2,1)S(1)} %get-tuple-element.33.refs_9_) | copy-start | bytes 12582916
  9.5 2.0 %copy-start.2 = (bf16[16,8,128,128]{3,2,1,0:T(8,128)(2,1)}, bf16[16,8,128,128]{3,2,1,0:T(8,128)(2,1)S(1)}, u32[]{:S(2)}) copy-start(bf16[16,8,128,128]{3,2,1,0:T(8,128)(2,1)S(1)} %get-tuple-element.34.refs_10_) | copy-start | bytes 12582916
  11.5 3.0 %collective-permute-start.3 = (bf16[128,1024]{1,0:T(8,128)(2,1)S(1)}, bf16[128,1024]{1,0:T(8,128)(2,1)S(1)}, u32[]{:S(2)}, u32[]{:S(2)}) collective-permute-start(bf16[128,1024]{1,0:T(8,128)(2,1)S(1)} %copy-done.8), channel_id=1, source_target_pairs={{0,1},{1,0},{2,3},{3,2},{4,5},{5,4},{6,7},{7,6},{8,9},{9,8},{10,11... | collective-permute-start | bytes 786440 | tf_op jit(solution)/shard_map/ppermute | solution.py:275
  12.8 6.3 %collective-permute-start.7 = (bf16[128,1024]{1,0:T(8,128)(2,1)}, bf16[128,1024]{1,0:T(8,128)(2,1)}, u32[]{:S(2)}, u32[]{:S(2)}) collective-permute-start(bf16[128,1024]{1,0:T(8,128)(2,1)} %collective-permute-done.2.refs_14_), channel_id=1, source_target_pairs={{0,1},{1,0},{2,3},{3,2},{4,5},{5,4},{6,7},{7,6},{8,9},{9,8},{10,11... | collective-permute-start | bytes 786440 | tf_op jit(solution)/shard_map/ppermute | solution.py:275
  12.9 21.1 %collective-permute-start.5 = (bf16[128,1024]{1,0:T(8,128)(2,1)S(1)}, bf16[128,1024]{1,0:T(8,128)(2,1)}, u32[]{:S(2)}, u32[]{:S(2)}) collective-permute-start(bf16[128,1024]{1,0:T(8,128)(2,1)S(1)} %copy-done.9), channel_id=1, source_target_pairs={{0,8},{4,12},{8,0},{12,4},{16,24},{20,28},{24,16},{28,20},{1,9},{5... | collective-permute-start | bytes 786440 | tf_op jit(solution)/shard_map/ppermute | solution.py:275
  14.2 20.6 %collective-permute-start.6 = (bf16[128,1024]{1,0:T(8,128)(2,1)S(1)}, bf16[128,1024]{1,0:T(8,128)(2,1)}, u32[]{:S(2)}, u32[]{:S(2)}) collective-permute-start(bf16[128,1024]{1,0:T(8,128)(2,1)S(1)} %copy-done.9), channel_id=1, source_target_pairs={{0,12},{4,8},{8,4},{12,0},{16,28},{20,24},{24,20},{28,16},{1,13},{... | collective-permute-start | bytes 786440 | tf_op jit(solution)/shard_map/ppermute | solution.py:275
  14.4 28.1 %collective-permute-start = (bf16[128,1024]{1,0:T(8,128)(2,1)S(1)}, bf16[128,1024]{1,0:T(8,128)(2,1)S(1)}, u32[]{:S(2)}, u32[]{:S(2)}) collective-permute-start(bf16[128,1024]{1,0:T(8,128)(2,1)S(1)} %copy-done.9), channel_id=1, source_target_pairs={{0,24},{4,28},{8,16},{12,20},{16,8},{20,12},{24,0},{28,4},{1,25},{... | collective-permute-start | bytes 786440 | tf_op jit(solution)/shard_map/ppermute | solution.py:275
  14.5 0.7 copy-start.10
  15.2 27.3 %collective-permute-start.4 = (bf16[128,1024]{1,0:T(8,128)(2,1)S(1)}, bf16[128,1024]{1,0:T(8,128)(2,1)S(1)}, u32[]{:S(2)}, u32[]{:S(2)}) collective-permute-start(bf16[128,1024]{1,0:T(8,128)(2,1)S(1)} %copy-done.9), channel_id=1, source_target_pairs={{0,16},{4,20},{8,24},{12,28},{16,0},{20,4},{24,8},{28,12},{1,17},{... | collective-permute-start | bytes 786440 | tf_op jit(solution)/shard_map/ppermute | solution.py:275
  19.2 2.2 %copy-start.1 = (bf16[16,8,128,128]{3,2,1,0:T(8,128)(2,1)S(1)}, bf16[16,8,128,128]{3,2,1,0:T(8,128)(2,1)}, u32[]{:S(2)}) copy-start(bf16[16,8,128,128]{3,2,1,0:T(8,128)(2,1)} %copy-done) | copy-start | bytes 12582916
  21.4 2.2 %copy-start.3 = (bf16[16,8,128,128]{3,2,1,0:T(8,128)(2,1)S(1)}, bf16[16,8,128,128]{3,2,1,0:T(8,128)(2,1)}, u32[]{:S(2)}) copy-start(bf16[16,8,128,128]{3,2,1,0:T(8,128)(2,1)} %copy-done.2) | copy-start | bytes 12582916
  23.6 1.6 %copy-start.5 = (bf16[1024,1024]{1,0:T(8,128)(2,1)S(1)}, bf16[1024,1024]{1,0:T(8,128)(2,1)}, u32[]{:S(2)}) copy-start(bf16[1024,1024]{1,0:T(8,128)(2,1)} %refs_8_.7) | copy-start | bytes 6291460
  25.1 1.6 %copy-start.7 = (bf16[1024,1024]{1,0:T(8,128)(2,1)S(1)}, bf16[1024,1024]{1,0:T(8,128)(2,1)}, u32[]{:S(2)}) copy-start(bf16[1024,1024]{1,0:T(8,128)(2,1)} %refs_11_.1) | copy-start | bytes 6291460
  26.7 0.9 %copy-start.11 = (bf16[128,1024]{1,0:T(8,128)(2,1)S(1)}, bf16[128,1024]{1,0:T(8,128)(2,1)}, u32[]{:S(2)}) copy-start(bf16[128,1024]{1,0:T(8,128)(2,1)} %copy-done.10) | copy-start | bytes 786436
  42.5 8.9 %collective-permute-start.8 = (bf16[128,1024]{1,0:T(8,128)(2,1)S(1)}, bf16[128,1024]{1,0:T(8,128)(2,1)S(1)}, u32[]{:S(2)}, u32[]{:S(2)}) collective-permute-start(bf16[128,1024]{1,0:T(8,128)(2,1)S(1)} %collective-permute-done.refs_5_), channel_id=1, source_target_pairs={{0,4},{4,0},{8,12},{12,8},{16,20},{20,16},{24,28},{28,24},{1,5},{5... | collective-permute-start | bytes 786440 | tf_op jit(solution)/shard_map/ppermute | solution.py:275
  42.6 8.8 %collective-permute-start.9 = (bf16[128,1024]{1,0:T(8,128)(2,1)S(1)}, bf16[128,1024]{1,0:T(8,128)(2,1)S(1)}, u32[]{:S(2)}, u32[]{:S(2)}) collective-permute-start(bf16[128,1024]{1,0:T(8,128)(2,1)S(1)} %collective-permute-done.4.refs_6_), channel_id=1, source_target_pairs={{0,4},{4,0},{8,12},{12,8},{16,20},{20,16},{24,28},{28,24},{1,5},{5... | collective-permute-start | bytes 786440 | tf_op jit(solution)/shard_map/ppermute | solution.py:275
  51.4 31.5 %copy-start.6 = (bf16[1024,1024]{1,0:T(8,128)(2,1)S(1)}, bf16[1024,1024]{1,0:T(8,128)(2,1)}, u32[]{:S(2)}) copy-start(bf16[1024,1024]{1,0:T(8,128)(2,1)} %refs_4_.9) | copy-start | bytes 6291460
  59.8 10.6 %collective-permute-start.10 = (bf16[1072,128]{1,0:T(8,128)(2,1)S(1)}, bf16[1072,128]{1,0:T(8,128)(2,1)S(1)}, u32[]{:S(2)}, u32[]{:S(2)}) collective-permute-start(bf16[1072,128]{1,0:T(8,128)(2,1)S(1)} %get-tuple-element.52), channel_id=1, source_target_pairs={{0,1},{1,0},{2,3},{3,2},{4,5},{5,4},{6,7},{7,6},{8,9},{9,8},{10,11... | collective-permute-start | bytes 823304 | tf_op jit(solution)/shard_map/ppermute | solution.py:275
  68.7 8.1 %collective-permute-start.11 = (bf16[1072,128]{1,0:T(8,128)(2,1)S(1)}, bf16[1072,128]{1,0:T(8,128)(2,1)S(1)}, u32[]{:S(2)}, u32[]{:S(2)}) collective-permute-start(bf16[1072,128]{1,0:T(8,128)(2,1)S(1)} %get-tuple-element.53), channel_id=1, source_target_pairs={{0,2},{1,3},{2,0},{3,1},{4,6},{5,7},{6,4},{7,5},{8,10},{9,11},{10,... | collective-permute-start | bytes 823304 | tf_op jit(solution)/shard_map/ppermute | solution.py:275
  68.7 14.2 %collective-permute-start.12 = (bf16[1072,128]{1,0:T(8,128)(2,1)S(1)}, bf16[1072,128]{1,0:T(8,128)(2,1)S(1)}, u32[]{:S(2)}, u32[]{:S(2)}) collective-permute-start(bf16[1072,128]{1,0:T(8,128)(2,1)S(1)} %get-tuple-element.54), channel_id=1, source_target_pairs={{0,3},{1,2},{2,1},{3,0},{4,7},{5,6},{6,5},{7,4},{8,11},{9,10},{10,... | collective-permute-start | bytes 823304 | tf_op jit(solution)/shard_map/ppermute | solution.py:275
